TPU v7x, 256 devices: a whole 4x4x8 slice. The times are simulated.
256 devices in a mesh: row: 32 (over x, y, core), feat: 8 (over z).
Axes of the slice: x: 4, y: 4, z: 8, core: 2. Of those that a mesh axis runs over, the one named last changes fastest.
Arguments:
- bins: int32 [1024, 262144], P('feat', 'row'), may hold values from 0 to 255
- grads: bfloat16 [262144], P('row'), may hold values from -6 to 6
- hess: bfloat16 [262144], P('row'), may hold values from 0.049804688 to 1
- node: int32 [262144], P('row'), may hold values from 0 to 7
Outputs:
- shortfall: float32 [1024, 8, 256], P(('feat', 'row'))
- best: float32 [8], replicated
All inputs are finite; a program needn't handle non-finite values.
Results may differ from a plain program's by a relative error of at most 0.0003.
Values sent between devices are 32-bit elements; how exact they have to be, the bound alone decides.
No kernel may reach another device: no remote copies, remote signals or barrier semaphores. Data moves between devices by JAX's collectives and lax.ppermute only.
A program may use at most 64 MiB of HBM per device.

v0:
```python
import jax
import jax.numpy as jnp
from jax import lax
from jax.sharding import PartitionSpec as P

BINS = 256
NODES = 8


def per_device(bins, grads, hess, node):
    feat_local = bins.shape[0]
    row_count = bins.shape[1]
    member = node[None, :] == jnp.arange(NODES, dtype=jnp.int32)[:, None]
    zero = jnp.zeros((), jnp.bfloat16)
    weighted = jnp.concatenate(
        [jnp.where(member, grads[None, :], zero), jnp.where(member, hess[None, :], zero)], axis=0
    )
    own_sums = jnp.sum(weighted.astype(jnp.float32), axis=1)
    node_sums = lax.psum(own_sums, "row")
    blocks = bins.reshape(feat_local // 8, 8, row_count)
    levels = jnp.arange(BINS, dtype=jnp.int32)

    def block_hist(columns):
        onehot = (columns[:, :, None] == levels[None, None, :]).astype(jnp.bfloat16)
        return jnp.einsum("kr,frb->fkb", weighted, onehot, preferred_element_type=jnp.float32)

    partial_hist = lax.map(block_hist, blocks).reshape(feat_local, 2 * NODES, BINS)
    summed = lax.psum(partial_hist, "row")
    share = feat_local // lax.axis_size("row")
    hist = lax.dynamic_slice_in_dim(summed, lax.axis_index("row") * share, share, 0)
    grad_total = node_sums[None, :NODES, None]
    hess_total = node_sums[None, NODES:, None]
    left = jnp.cumsum(hist, axis=2)
    grad_left = left[:, :NODES]
    hess_left = left[:, NODES:]
    gain = grad_left * grad_left / (hess_left + 1.0)
    gain = gain + (grad_total - grad_left) ** 2 / (hess_total - hess_left + 1.0)
    gain = gain - grad_total * grad_total / (hess_total + 1.0)
    local_best = jnp.max(gain, axis=(0, 2))
    best = lax.pmax(local_best, ("row", "feat"))
    return (gain - best[None, :, None], best)


def solution(mesh):
    return jax.shard_map(
        per_device,
        mesh=mesh,
        in_specs=(P("feat", "row"), P("row"), P("row"), P("row")),
        out_specs=(P(("feat", "row"), None, None), P()),
        check_vma=False,
    )
```

profile of v0, /device:TPU:1, one launch (start us, length us, event | category | flops | bytes accessed | tf_op | source)
XLA Modules:
  0.0 433.2 jit_solution(3313179824305272989)
XLA Ops:
  8.1 215.5 %while.11 = (s32[]{:T(128)}, f32[16,8,16,256]{3,2,1,0:T(8,128)}, s32[16,8,8192]{2,1,0:T(8,128)}, bf16[16,8192]{1,0:T(8,128)(2,1)S(1)}, s32[]{:T(128)}) while((s32[]{:T(128)}, f32[16,8,16,256]{3,2,1,0:T(8,128)}, s32[16,8,8192]{2,1,0:T(8,128)}, bf16[16,8192]{1,0:T(8,128)(2,1)S(1)}, s32[]{:T(128)}) %tuple.34), condition=%wide.region_1.2_spmd.clone, body=%wide.region_0.1_spmd.clone.sunk | while | flops 553648128 | bytes 1179725 | solution.py:27
  8.1 1.0 dynamic-slice_bitcast_fusion.4
  9.1 12.5 %fusion.17 = f32[16,8,16,256]{3,2,1,0:T(8,128)} fusion(f32[16,8,16,256]{3,2,1,0:T(8,128)} %get-tuple-element.86, s32[]{:T(128)S(6)} %copy.19, s32[8,8192]{1,0:T(8,128)S(1)} %dynamic-slice_bitcast_fusion.4, bf16[16,8192]{1,0:T(8,128)(2,1)S(1)} %get-tuple-element.93), kind=kOutput, calls=%fused_computation.5.clone.2 | convolution fusion | flops 553648128 | bytes 655364 | tf_op jit(solution)/shard_map/while/body/eval_jaxpr/kr,frb->fkb/dot_general | solution.py:25
  21.6 1.0 dynamic-slice_bitcast_fusion.4
  22.5 12.5 %fusion.17 = f32[16,8,16,256]{3,2,1,0:T(8,128)} fusion(f32[16,8,16,256]{3,2,1,0:T(8,128)} %get-tuple-element.86, s32[]{:T(128)S(6)} %copy.19, s32[8,8192]{1,0:T(8,128)S(1)} %dynamic-slice_bitcast_fusion.4, bf16[16,8192]{1,0:T(8,128)(2,1)S(1)} %get-tuple-element.93), kind=kOutput, calls=%fused_computation.5.clone.2 | convolution fusion | flops 553648128 | bytes 655364 | tf_op jit(solution)/shard_map/while/body/eval_jaxpr/kr,frb->fkb/dot_general | solution.py:25
  35.0 1.0 dynamic-slice_bitcast_fusion.4
  36.0 12.5 %fusion.17 = f32[16,8,16,256]{3,2,1,0:T(8,128)} fusion(f32[16,8,16,256]{3,2,1,0:T(8,128)} %get-tuple-element.86, s32[]{:T(128)S(6)} %copy.19, s32[8,8192]{1,0:T(8,128)S(1)} %dynamic-slice_bitcast_fusion.4, bf16[16,8192]{1,0:T(8,128)(2,1)S(1)} %get-tuple-element.93), kind=kOutput, calls=%fused_computation.5.clone.2 | convolution fusion | flops 553648128 | bytes 655364 | tf_op jit(solution)/shard_map/while/body/eval_jaxpr/kr,frb->fkb/dot_general | solution.py:25
  48.5 1.0 dynamic-slice_bitcast_fusion.4
  49.5 12.5 %fusion.17 = f32[16,8,16,256]{3,2,1,0:T(8,128)} fusion(f32[16,8,16,256]{3,2,1,0:T(8,128)} %get-tuple-element.86, s32[]{:T(128)S(6)} %copy.19, s32[8,8192]{1,0:T(8,128)S(1)} %dynamic-slice_bitcast_fusion.4, bf16[16,8192]{1,0:T(8,128)(2,1)S(1)} %get-tuple-element.93), kind=kOutput, calls=%fused_computation.5.clone.2 | convolution fusion | flops 553648128 | bytes 655364 | tf_op jit(solution)/shard_map/while/body/eval_jaxpr/kr,frb->fkb/dot_general | solution.py:25
  62.0 1.0 dynamic-slice_bitcast_fusion.4
  62.9 12.5 %fusion.17 = f32[16,8,16,256]{3,2,1,0:T(8,128)} fusion(f32[16,8,16,256]{3,2,1,0:T(8,128)} %get-tuple-element.86, s32[]{:T(128)S(6)} %copy.19, s32[8,8192]{1,0:T(8,128)S(1)} %dynamic-slice_bitcast_fusion.4, bf16[16,8192]{1,0:T(8,128)(2,1)S(1)} %get-tuple-element.93), kind=kOutput, calls=%fused_computation.5.clone.2 | convolution fusion | flops 553648128 | bytes 655364 | tf_op jit(solution)/shard_map/while/body/eval_jaxpr/kr,frb->fkb/dot_general | solution.py:25
  75.4 1.0 dynamic-slice_bitcast_fusion.4
  76.4 12.5 %fusion.17 = f32[16,8,16,256]{3,2,1,0:T(8,128)} fusion(f32[16,8,16,256]{3,2,1,0:T(8,128)} %get-tuple-element.86, s32[]{:T(128)S(6)} %copy.19, s32[8,8192]{1,0:T(8,128)S(1)} %dynamic-slice_bitcast_fusion.4, bf16[16,8192]{1,0:T(8,128)(2,1)S(1)} %get-tuple-element.93), kind=kOutput, calls=%fused_computation.5.clone.2 | convolution fusion | flops 553648128 | bytes 655364 | tf_op jit(solution)/shard_map/while/body/eval_jaxpr/kr,frb->fkb/dot_general | solution.py:25
  88.9 1.0 dynamic-slice_bitcast_fusion.4
  89.9 12.5 %fusion.17 = f32[16,8,16,256]{3,2,1,0:T(8,128)} fusion(f32[16,8,16,256]{3,2,1,0:T(8,128)} %get-tuple-element.86, s32[]{:T(128)S(6)} %copy.19, s32[8,8192]{1,0:T(8,128)S(1)} %dynamic-slice_bitcast_fusion.4, bf16[16,8192]{1,0:T(8,128)(2,1)S(1)} %get-tuple-element.93), kind=kOutput, calls=%fused_computation.5.clone.2 | convolution fusion | flops 553648128 | bytes 655364 | tf_op jit(solution)/shard_map/while/body/eval_jaxpr/kr,frb->fkb/dot_general | solution.py:25
  102.4 1.0 dynamic-slice_bitcast_fusion.4
  103.3 12.5 %fusion.17 = f32[16,8,16,256]{3,2,1,0:T(8,128)} fusion(f32[16,8,16,256]{3,2,1,0:T(8,128)} %get-tuple-element.86, s32[]{:T(128)S(6)} %copy.19, s32[8,8192]{1,0:T(8,128)S(1)} %dynamic-slice_bitcast_fusion.4, bf16[16,8192]{1,0:T(8,128)(2,1)S(1)} %get-tuple-element.93), kind=kOutput, calls=%fused_computation.5.clone.2 | convolution fusion | flops 553648128 | bytes 655364 | tf_op jit(solution)/shard_map/while/body/eval_jaxpr/kr,frb->fkb/dot_general | solution.py:25
  115.8 1.0 dynamic-slice_bitcast_fusion.4
  116.8 12.5 %fusion.17 = f32[16,8,16,256]{3,2,1,0:T(8,128)} fusion(f32[16,8,16,256]{3,2,1,0:T(8,128)} %get-tuple-element.86, s32[]{:T(128)S(6)} %copy.19, s32[8,8192]{1,0:T(8,128)S(1)} %dynamic-slice_bitcast_fusion.4, bf16[16,8192]{1,0:T(8,128)(2,1)S(1)} %get-tuple-element.93), kind=kOutput, calls=%fused_computation.5.clone.2 | convolution fusion | flops 553648128 | bytes 655364 | tf_op jit(solution)/shard_map/while/body/eval_jaxpr/kr,frb->fkb/dot_general | solution.py:25
  129.3 1.0 dynamic-slice_bitcast_fusion.4
  130.3 12.5 %fusion.17 = f32[16,8,16,256]{3,2,1,0:T(8,128)} fusion(f32[16,8,16,256]{3,2,1,0:T(8,128)} %get-tuple-element.86, s32[]{:T(128)S(6)} %copy.19, s32[8,8192]{1,0:T(8,128)S(1)} %dynamic-slice_bitcast_fusion.4, bf16[16,8192]{1,0:T(8,128)(2,1)S(1)} %get-tuple-element.93), kind=kOutput, calls=%fused_computation.5.clone.2 | convolution fusion | flops 553648128 | bytes 655364 | tf_op jit(solution)/shard_map/while/body/eval_jaxpr/kr,frb->fkb/dot_general | solution.py:25
  142.8 1.0 dynamic-slice_bitcast_fusion.4
  143.8 12.5 %fusion.17 = f32[16,8,16,256]{3,2,1,0:T(8,128)} fusion(f32[16,8,16,256]{3,2,1,0:T(8,128)} %get-tuple-element.86, s32[]{:T(128)S(6)} %copy.19, s32[8,8192]{1,0:T(8,128)S(1)} %dynamic-slice_bitcast_fusion.4, bf16[16,8192]{1,0:T(8,128)(2,1)S(1)} %get-tuple-element.93), kind=kOutput, calls=%fused_computation.5.clone.2 | convolution fusion | flops 553648128 | bytes 655364 | tf_op jit(solution)/shard_map/while/body/eval_jaxpr/kr,frb->fkb/dot_general | solution.py:25
  157.2 12.5 %fusion.17 = f32[16,8,16,256]{3,2,1,0:T(8,128)} fusion(f32[16,8,16,256]{3,2,1,0:T(8,128)} %get-tuple-element.86, s32[]{:T(128)S(6)} %copy.19, s32[8,8192]{1,0:T(8,128)S(1)} %dynamic-slice_bitcast_fusion.4, bf16[16,8192]{1,0:T(8,128)(2,1)S(1)} %get-tuple-element.93), kind=kOutput, calls=%fused_computation.5.clone.2 | convolution fusion | flops 553648128 | bytes 655364 | tf_op jit(solution)/shard_map/while/body/eval_jaxpr/kr,frb->fkb/dot_general | solution.py:25
  170.7 12.5 %fusion.17 = f32[16,8,16,256]{3,2,1,0:T(8,128)} fusion(f32[16,8,16,256]{3,2,1,0:T(8,128)} %get-tuple-element.86, s32[]{:T(128)S(6)} %copy.19, s32[8,8192]{1,0:T(8,128)S(1)} %dynamic-slice_bitcast_fusion.4, bf16[16,8192]{1,0:T(8,128)(2,1)S(1)} %get-tuple-element.93), kind=kOutput, calls=%fused_computation.5.clone.2 | convolution fusion | flops 553648128 | bytes 655364 | tf_op jit(solution)/shard_map/while/body/eval_jaxpr/kr,frb->fkb/dot_general | solution.py:25
  184.2 12.5 %fusion.17 = f32[16,8,16,256]{3,2,1,0:T(8,128)} fusion(f32[16,8,16,256]{3,2,1,0:T(8,128)} %get-tuple-element.86, s32[]{:T(128)S(6)} %copy.19, s32[8,8192]{1,0:T(8,128)S(1)} %dynamic-slice_bitcast_fusion.4, bf16[16,8192]{1,0:T(8,128)(2,1)S(1)} %get-tuple-element.93), kind=kOutput, calls=%fused_computation.5.clone.2 | convolution fusion | flops 553648128 | bytes 655364 | tf_op jit(solution)/shard_map/while/body/eval_jaxpr/kr,frb->fkb/dot_general | solution.py:25
  197.6 12.5 %fusion.17 = f32[16,8,16,256]{3,2,1,0:T(8,128)} fusion(f32[16,8,16,256]{3,2,1,0:T(8,128)} %get-tuple-element.86, s32[]{:T(128)S(6)} %copy.19, s32[8,8192]{1,0:T(8,128)S(1)} %dynamic-slice_bitcast_fusion.4, bf16[16,8192]{1,0:T(8,128)(2,1)S(1)} %get-tuple-element.93), kind=kOutput, calls=%fused_computation.5.clone.2 | convolution fusion | flops 553648128 | bytes 655364 | tf_op jit(solution)/shard_map/while/body/eval_jaxpr/kr,frb->fkb/dot_general | solution.py:25
  211.1 12.5 %fusion.17 = f32[16,8,16,256]{3,2,1,0:T(8,128)} fusion(f32[16,8,16,256]{3,2,1,0:T(8,128)} %get-tuple-element.86, s32[]{:T(128)S(6)} %copy.19, s32[8,8192]{1,0:T(8,128)S(1)} %dynamic-slice_bitcast_fusion.4, bf16[16,8192]{1,0:T(8,128)(2,1)S(1)} %get-tuple-element.93), kind=kOutput, calls=%fused_computation.5.clone.2 | convolution fusion | flops 553648128 | bytes 655364 | tf_op jit(solution)/shard_map/while/body/eval_jaxpr/kr,frb->fkb/dot_general | solution.py:25
  223.8 65.6 %psum.15 = f32[16]{0:T(128)S(1)} all-reduce(f32[16]{0:T(128)S(1)} %convert_reduce_fusion), channel_id=1, replica_groups=mesh['row'=32,'feat'=8] {'row'}, use_global_device_ids=true, to_apply=%region_6.7 | all-reduce | flops 16 | bytes 128 | tf_op jit(solution)/shard_map/psum | solution.py:19
  289.4 55.6 %all-reduce.2.cloned.1.call-done = f32[128,16,256]{2,1,0:T(8,128)} async-done(((f32[128,16,256]{2,1,0:T(8,128)}), f32[128,16,256]{2,1,0:T(8,128)}) %all-reduce.2.cloned.1.call-update) | async-done | bytes 2097168 | tf_op jit(solution)/shard_map/psum | solution.py:28
  345.9 2.3 reduce-window.6
  348.7 77.0 %pmax.7 = f32[8]{0:T(128)S(1)} all-reduce(f32[8]{0:T(128)S(1)} %get-tuple-element.48), channel_id=1, replica_groups=mesh['row'=32,'feat'=8] {'row','feat'}, use_global_device_ids=true, to_apply=%region_8.9 | all-reduce | flops 8 | bytes 64 | tf_op jit(solution)/shard_map/pmax | solution.py:40
  (23 shorter events, 8.0 us)
Async XLA Ops:
  7.2 337.9 %all-reduce.2.cloned.1.call-start = ((), (), s32[]{:S(2)}) async-start(), calls=%async_computation | async-start | bytes 4194304 | tf_op jit(solution)/shard_map/psum | solution.py:28
  425.7 0.7 copy-start
Sparse Core Ops, SparseCore 0:
  223.8 121.2 all-reduce.1
where the time goes:
time: 434 us; the launch traced here: 433 us
  matrix products  200 us (46%)
  blocking collectives  143 us (33%)
  waiting for transfers between devices  55.6 us (13%)
  local copies, waits for them, and re-layouts  16.5 us (4%)
  between operations  14.1 us (3%)
  other arithmetic  4.36 us (1%)
    dot_general x16, matrix products, block_hist(): jnp.einsum('kr,frb->fkb', weighted, onehot, preferred_element_type=jnp.fl...  200 us
    pmax x1, blocking collectives, per_device(): best = lax.pmax(local_best, ('row', 'feat'))  77 us
    psum x1, blocking collectives, per_device(): node_sums = lax.psum(own_sums, 'row')  65.6 us
    psum x1, waiting for transfers between devices, per_device(): summed = lax.psum(partial_hist, 'row')  55.6 us
    eq x16, local copies, waits for them, and re-layouts, block_hist(): onehot = (columns[:, :, None] == levels[None, None, :]).astype(jnp.bfloat16)  15.5 us
  transfers between devices with their start and end apart: 1, of which 1 were waited for; matrix products, arithmetic and copies ran while one was open for 0% of the time, Pallas kernels for 0%

commit v1 on v0

v1 whole, which is shorter than its diff:
```python
import functools

import jax
import jax.numpy as jnp
from jax import lax
from jax.experimental import pallas as pl
from jax.experimental.pallas import tpu as pltpu
from jax.sharding import PartitionSpec as P

BINS = 256
NODES = 8
STATS = 2 * NODES
LOW = 64
HIGH = BINS // LOW
GROUP = BINS // LOW
SUB = 8
CHUNK = 512


def hist_kernel(bins_ref, weighted_ref, out_ref):
    rows = bins_ref.shape[1]
    level = lax.broadcasted_iota(jnp.int32, (STATS, CHUNK), 0)
    zero = jnp.zeros((), jnp.bfloat16)
    one = jnp.ones((), jnp.bfloat16)
    for group in range(SUB // GROUP):
        total = jnp.zeros((GROUP * HIGH * STATS, GROUP * LOW), jnp.float32)
        for chunk in range(rows // CHUNK):
            at = slice(chunk * CHUNK, (chunk + 1) * CHUNK)
            columns = bins_ref[group * GROUP : (group + 1) * GROUP, at]
            weighted = weighted_ref[:, at]
            low = columns & (LOW - 1)
            high = columns >> (LOW.bit_length() - 1)
            left = []
            right = []
            for j in range(GROUP):
                low_j = jnp.broadcast_to(low[j : j + 1].astype(jnp.bfloat16), (STATS, CHUNK))
                for i in range(LOW // STATS):
                    wanted = (level + STATS * i).astype(jnp.bfloat16)
                    right.append(jnp.where(low_j == wanted, one, zero))
                high_j = jnp.broadcast_to(high[j : j + 1].astype(jnp.bfloat16), (STATS, CHUNK))
                for q in range(HIGH):
                    left.append(jnp.where(high_j == jnp.asarray(q, jnp.bfloat16), weighted, zero))
            total = total + lax.dot_general(
                jnp.concatenate(left, 0),
                jnp.concatenate(right, 0),
                (((1,), (1,)), ((), ())),
                preferred_element_type=jnp.float32,
            )
        for j in range(GROUP):
            blocks = [
                total[(j * HIGH + q) * STATS : (j * HIGH + q + 1) * STATS, j * LOW : (j + 1) * LOW]
                for q in range(HIGH)
            ]
            out_ref[group * GROUP + j] = jnp.concatenate(blocks, axis=1)


def histogram(bins, weighted):
    features, rows = bins.shape
    return pl.pallas_call(
        hist_kernel,
        grid=(features // SUB,),
        in_specs=[pl.BlockSpec((SUB, rows), lambda i: (i, 0)), pl.BlockSpec((STATS, rows), lambda i: (0, 0))],
        out_specs=pl.BlockSpec((SUB, STATS, BINS), lambda i: (i, 0, 0)),
        out_shape=jax.ShapeDtypeStruct((features, STATS, BINS), jnp.float32),
        compiler_params=pltpu.CompilerParams(vmem_limit_bytes=48 * 2**20),
        cost_estimate=pl.CostEstimate(
            flops=2 * features * rows * STATS * BINS, bytes_accessed=4 * features * rows, transcendentals=0
        ),
        name="histogram",
    )(bins, weighted)


def gain_kernel(parts_ref, gain_ref, best_ref):
    count = parts_ref.shape[0]
    hist = parts_ref[0]
    for i in range(1, count):
        hist = hist + parts_ref[i]
    upper = lax.broadcasted_iota(jnp.int32, (BINS, BINS), 0) <= lax.broadcasted_iota(jnp.int32, (BINS, BINS), 1)
    left = lax.dot_general(
        hist,
        upper.astype(jnp.float32),
        (((1,), (0,)), ((), ())),
        precision=lax.Precision.HIGHEST,
        preferred_element_type=jnp.float32,
    )
    best = None
    for f in range(gain_ref.shape[0]):
        grad_left = left[f * STATS : f * STATS + NODES]
        hess_left = left[f * STATS + NODES : (f + 1) * STATS]
        grad_total = grad_left[:, BINS - 1 :]
        hess_total = hess_left[:, BINS - 1 :]
        gain = grad_left * grad_left / (hess_left + 1.0)
        gain = gain + (grad_total - grad_left) ** 2 / (hess_total - hess_left + 1.0)
        gain = gain - grad_total * grad_total / (hess_total + 1.0)
        gain_ref[f] = gain
        most = jnp.max(gain, axis=1, keepdims=True)
        best = most if best is None else jnp.maximum(best, most)
    best_ref[...] = jnp.broadcast_to(best, best_ref.shape)


def gains(parts):
    share = parts.shape[1]
    count = parts.shape[0]
    return pl.pallas_call(
        gain_kernel,
        out_shape=(
            jax.ShapeDtypeStruct((share, NODES, BINS), jnp.float32),
            jax.ShapeDtypeStruct((NODES, 128), jnp.float32),
        ),
        compiler_params=pltpu.CompilerParams(vmem_limit_bytes=48 * 2**20),
        name="gains",
    )(parts.reshape(count, share * STATS, BINS))


def per_device(bins, grads, hess, node):
    features = bins.shape[0]
    row_size = lax.axis_size("row")
    device_count = row_size * lax.axis_size("feat")
    share = features // row_size
    member = node[None, :] == jnp.arange(NODES, dtype=jnp.int32)[:, None]
    zero = jnp.zeros((), jnp.bfloat16)
    weighted = jnp.concatenate(
        [jnp.where(member, grads[None, :], zero), jnp.where(member, hess[None, :], zero)], axis=0
    )
    partial_hist = histogram(bins, weighted)
    parts = lax.all_to_all(partial_hist.reshape(row_size, share, STATS, BINS), "row", 0, 0)
    gain, own_best = gains(parts)
    copies = jnp.broadcast_to(own_best[None, :, 0], (device_count, NODES))
    best = jnp.max(lax.all_to_all(copies, ("row", "feat"), 0, 0), axis=0)
    return (gain - best[None, :, None], best)


def solution(mesh):
    return jax.shard_map(
        per_device,
        mesh=mesh,
        in_specs=(P("feat", "row"), P("row"), P("row"), P("row")),
        out_specs=(P(("feat", "row"), None, None), P()),
        check_vma=False,
    )
```

time: 434 us -> 104 us (0.24)
  matrix products: 200 us -> 0 us
  blocking collectives: 143 us -> 60.4 us
  waiting for transfers between devices: 55.6 us -> 0 us
  Pallas kernels: 0 us -> 40.4 us
  local copies, waits for them, and re-layouts: 16.5 us -> 0.2 us
  between operations: 14.1 us -> 0.67 us
    dot_general x16 -> x0, matrix products: 200 us -> none  [block_hist(): jnp.einsum('kr,frb->fkb', weighted, onehot, preferred_element_type=jnp.fl...]
    pmax x1 -> x0, blocking collectives: 77 us -> none  [per_device(): best = lax.pmax(local_best, ('row', 'feat'))]
    psum x1 -> x0, blocking collectives: 65.6 us -> none  [per_device(): node_sums = lax.psum(own_sums, 'row')]
    all_to_all x0 -> x2, blocking collectives: none -> 60.4 us  [the longest x1 36.5 us: per_device(): lax.all_to_all(partial_hist.reshape(row_size, share, STATS, BINS), 'row',...]
    psum x1 -> x0, waiting for transfers between devices: 55.6 us -> none  [per_device(): summed = lax.psum(partial_hist, 'row')]
    pallas_call x0 -> x2, Pallas kernels: none -> 40.4 us  [the longest x1 39.9 us: histogram(): pl.pallas_call(hist_kernel, grid=(features // SUB,), in_specs=[pl.BlockSp...]
    eq x16 -> x0, local copies, waits for them, and re-layouts: 15.5 us -> none  [block_hist(): onehot = (columns[:, :, None] == levels[None, None, :]).astype(jnp.bfloat16)]
  transfers between devices with their start and end apart: 1 -> 0, of which waited for: 1 -> 0; matrix products, arithmetic and copies ran while one was open for 0% -> 0% of each run, Pallas kernels for 0% -> 0%
where the time goes in v1:
time: 104 us; the launch traced here: 103 us
  blocking collectives  60.4 us (58%)
  Pallas kernels  40.4 us (39%)
  other arithmetic  1.82 us (2%)
    pallas_call x1, Pallas kernels, histogram(): pl.pallas_call(hist_kernel, grid=(features // SUB,), in_specs=[pl.BlockSp...  39.9 us
    all_to_all x1, blocking collectives, per_device(): lax.all_to_all(partial_hist.reshape(row_size, share, STATS, BINS), 'row',...  36.5 us
    all_to_all x1, blocking collectives, per_device(): best = jnp.max(lax.all_to_all(copies, ('row', 'feat'), 0, 0), axis=0)  23.9 us

profile of v1, /device:TPU:1, one launch (start us, length us, event | category | flops | bytes accessed | tf_op | source)
XLA Modules:
  0.0 103.5 jit_solution(14954383237879738281)
XLA Ops:
  0.6 0.8 fusion.1
  1.5 39.9 %histogram.1 = f32[128,16,256]{2,1,0:T(8,128)S(1)} custom-call(s32[128,8192]{1,0:T(8,128)} %bins_ref.1, bf16[16,8192]{1,0:T(8,128)(2,1)S(1)} %pad_maximum_fusion.weighted_ref), custom_call_target="tpu_custom_call" | custom-call | flops 8589934592 | bytes 4194304 | tf_op jit(solution)/shard_map/histogram/pallas_call | solution.py:59
  41.4 36.5 %all_to_all.11 = f32[32,4,16,256]{3,2,1,0:T(8,128)S(1)} all-to-all(f32[32,4,16,256]{3,2,1,0:T(8,128)S(1)} %bitcast.3), channel_id=1, replica_groups=mesh['row'=32,'feat'=8] {'row'}, dimensions={0} | all-to-all | bytes 4194304 | tf_op jit(solution)/shard_map/all_to_all | solution.py:126
  77.9 0.5 gains.1
  78.4 0.1 slice_reduce_fusion
  78.5 0.1 broadcast_in_dim.34
  78.6 23.9 %all_to_all.12 = f32[256,1,8]{2,1,0:T(1,128)S(1)} all-to-all(f32[256,1,8]{2,1,0:T(1,128)S(1)} %broadcast_in_dim.34), channel_id=1, replica_groups=mesh['row'=32,'feat'=8] {'row','feat'}, dimensions={0} | all-to-all | bytes 16384 | tf_op jit(solution)/shard_map/all_to_all | solution.py:129
  102.5 0.3 reduce_max.9
  102.8 0.0 copy-start
  102.8 0.7 broadcast_subtract_fusion
  103.5 0.0 copy-done
  (1 shorter events, 0.0 us)
Async XLA Ops:
  102.8 0.7 copy-start

commit v2 on v1

v2 whole, which is shorter than its diff:
```python
import functools

import jax
import jax.numpy as jnp
from jax import lax
from jax.experimental import pallas as pl
from jax.experimental.pallas import tpu as pltpu
from jax.sharding import PartitionSpec as P

BINS = 256
NODES = 8
STATS = 2 * NODES
LOW = 64
HIGH = BINS // LOW
GROUP = BINS // LOW
SUB = 16
CHUNK = 512
SHARE = 4
CORES = 2
PIECES = ((0, 1), (2, 3))


def hist_kernel(picks, core_ref, bins_ref, weighted_ref, keep_ref, send_ref, held_ref):
    rows = bins_ref.shape[1]
    core = core_ref[0]
    level = lax.broadcasted_iota(jnp.int32, (STATS, CHUNK), 0)
    zero = jnp.zeros((), jnp.bfloat16)
    one = jnp.ones((), jnp.bfloat16)
    features = [(owner, slot) for owner in range(SUB // SHARE) for slot in range(len(picks))]
    for first in range(0, len(features), GROUP):
        group = features[first : first + GROUP]
        total = jnp.zeros((GROUP * HIGH * STATS, GROUP * LOW), jnp.float32)
        for chunk in range(rows // CHUNK):
            at = slice(chunk * CHUNK, (chunk + 1) * CHUNK)
            weighted = weighted_ref[:, at]
            left = []
            right = []
            for owner, slot in group:
                column = bins_ref[owner * SHARE + picks[slot] : owner * SHARE + picks[slot] + 1, at]
                low = (column & (LOW - 1)).astype(jnp.bfloat16)
                high = (column >> (LOW.bit_length() - 1)).astype(jnp.bfloat16)
                low = jnp.broadcast_to(low, (STATS, CHUNK))
                for i in range(LOW // STATS):
                    wanted = (level + STATS * i).astype(jnp.bfloat16)
                    right.append(jnp.where(low == wanted, one, zero))
                high = jnp.broadcast_to(high, (STATS, CHUNK))
                for q in range(HIGH):
                    left.append(jnp.where(high == jnp.asarray(q, jnp.bfloat16), weighted, zero))
            total = total + lax.dot_general(
                jnp.concatenate(left, 0),
                jnp.concatenate(right, 0),
                (((1,), (1,)), ((), ())),
                preferred_element_type=jnp.float32,
            )
        for j, (owner, slot) in enumerate(group):
            blocks = [
                total[(j * HIGH + q) * STATS : (j * HIGH + q + 1) * STATS, j * LOW : (j + 1) * LOW]
                for q in range(HIGH)
            ]
            held_ref[owner, slot] = jnp.concatenate(blocks, axis=1)
    for chip in range(SUB // SHARE // CORES):
        first, second = held_ref[chip * CORES], held_ref[chip * CORES + 1]
        keep_ref[chip] = jnp.where(core == 0, first, second)
        send_ref[chip] = jnp.where(core == 0, second, first)


def histogram(bins, weighted, core, picks):
    features, rows = bins.shape
    chips = features // (SHARE * CORES)
    step = SUB // (SHARE * CORES)
    count = len(picks)
    return pl.pallas_call(
        functools.partial(hist_kernel, picks),
        grid=(features // SUB,),
        in_specs=[
            pl.BlockSpec(memory_space=pltpu.SMEM),
            pl.BlockSpec((SUB, rows), lambda i: (i, 0)),
            pl.BlockSpec((STATS, rows), lambda i: (0, 0)),
        ],
        out_specs=[pl.BlockSpec((step, count, STATS, BINS), lambda i: (i, 0, 0, 0))] * 2,
        out_shape=[jax.ShapeDtypeStruct((chips, count, STATS, BINS), jnp.float32)] * 2,
        scratch_shapes=[pltpu.VMEM((SUB // SHARE, count, STATS, BINS), jnp.float32)],
        compiler_params=pltpu.CompilerParams(vmem_limit_bytes=60 * 2**20),
        cost_estimate=pl.CostEstimate(
            flops=2 * features * count // SHARE * rows * LOW * BINS,
            bytes_accessed=4 * features * rows,
            transcendentals=0,
        ),
        name="histogram",
    )(core, bins, weighted)


def gain_kernel(*refs):
    parts, (gain_ref, best_ref) = refs[: len(PIECES)], refs[len(PIECES) :]
    upper = lax.broadcasted_iota(jnp.int32, (BINS, BINS), 0) <= lax.broadcasted_iota(jnp.int32, (BINS, BINS), 1)
    upper = upper.astype(jnp.float32)
    best = None
    for picks, ref in zip(PIECES, parts):
        hist = ref[0]
        for i in range(1, ref.shape[0]):
            hist = hist + ref[i]
        left = lax.dot_general(
            hist,
            upper,
            (((1,), (0,)), ((), ())),
            precision=lax.Precision.HIGHEST,
            preferred_element_type=jnp.float32,
        )
        for slot, feature in enumerate(picks):
            grad_left = left[slot * STATS : slot * STATS + NODES]
            hess_left = left[slot * STATS + NODES : (slot + 1) * STATS]
            grad_total = grad_left[:, BINS - 1 :]
            hess_total = hess_left[:, BINS - 1 :]
            gain = grad_left * grad_left / (hess_left + 1.0)
            gain = gain + (grad_total - grad_left) ** 2 / (hess_total - hess_left + 1.0)
            gain = gain - grad_total * grad_total / (hess_total + 1.0)
            gain_ref[feature] = gain
            most = jnp.max(gain, axis=1, keepdims=True)
            best = most if best is None else jnp.maximum(best, most)
    best_ref[...] = jnp.broadcast_to(best, best_ref.shape)


def gains(*parts):
    parts = [p.reshape(p.shape[0], p.shape[1] * STATS, BINS) for p in parts]
    return pl.pallas_call(
        gain_kernel,
        out_shape=(
            jax.ShapeDtypeStruct((SHARE, NODES, BINS), jnp.float32),
            jax.ShapeDtypeStruct((NODES, 128), jnp.float32),
        ),
        compiler_params=pltpu.CompilerParams(vmem_limit_bytes=60 * 2**20),
        name="gains",
    )(*parts)


def per_device(bins, grads, hess, node):
    row_size = lax.axis_size("row")
    feat_size = lax.axis_size("feat")
    chips = row_size // CORES
    swap = [(i, i ^ 1) for i in range(row_size)]
    same_core = [[chip * CORES + c for chip in range(chips)] for c in range(CORES)]
    same_core_all = [[i * feat_size + z for i in group for z in range(feat_size)] for group in same_core]
    member = node[None, :] == jnp.arange(NODES, dtype=jnp.int32)[:, None]
    zero = jnp.zeros((), jnp.bfloat16)
    weighted = jnp.concatenate(
        [jnp.where(member, grads[None, :], zero), jnp.where(member, hess[None, :], zero)], axis=0
    )
    core = (lax.axis_index("row") % CORES)[None]
    parts = []
    for picks in PIECES:
        keep, send = histogram(bins, weighted, core, picks)
        if parts:
            send, parts[-1] = lax.optimization_barrier((send, parts[-1]))
        pair = keep + lax.ppermute(send, "row", swap)
        pair, weighted = lax.optimization_barrier((pair, weighted))
        parts.append(lax.all_to_all(pair, "row", 0, 0, axis_index_groups=same_core, tiled=True))
    gain, own_best = gains(*parts)
    own_best = own_best[:, 0]
    own_best = jnp.maximum(own_best, lax.ppermute(own_best, "row", swap))
    copies = jnp.broadcast_to(own_best, (chips * feat_size, NODES))
    best = jnp.max(lax.all_to_all(copies, ("row", "feat"), 0, 0, axis_index_groups=same_core_all, tiled=True), axis=0)
    return (gain - best[None, :, None], best)


def solution(mesh):
    return jax.shard_map(
        per_device,
        mesh=mesh,
        in_specs=(P("feat", "row"), P("row"), P("row"), P("row")),
        out_specs=(P(("feat", "row"), None, None), P()),
        check_vma=False,
    )
```

time: 104 us -> 108 us (1.038)
  blocking collectives: 60.4 us -> 39.4 us
  starting transfers between devices: 0 us -> 11.2 us
  Pallas kernels: 40.4 us -> 45 us
  other arithmetic: 1.82 us -> 6.18 us
  waiting for transfers between devices: 0 us -> 4.32 us
    all_to_all x2, blocking collectives: 60.4 us -> 39.4 us  [the longest x1 22.2 us: per_device(): lax.all_to_all(copies, ('row', 'feat'), 0, 0, axis_index_groups=same_core...]
    ppermute x0 -> x3, starting transfers between devices: none -> 6.19 us  [the longest x2 4.02 us: per_device(): pair = keep + lax.ppermute(send, 'row', swap)]
    all_to_all x0 -> x1, starting transfers between devices: none -> 5.02 us  [per_device(): lax.all_to_all(pair, 'row', 0, 0, axis_index_groups=same_core, tiled=True)]
    pallas_call x2 -> x3, Pallas kernels: 40.4 us -> 45 us  [the longest x2 42.7 us: histogram(): pl.pallas_call(functools.partial(hist_kernel, picks), grid=(features // S...]
    ppermute x0 -> x3, waiting for transfers between devices: none -> 4.31 us  [the longest x2 3.49 us: per_device(): pair = keep + lax.ppermute(send, 'row', swap)]
    add x0 -> x2, other arithmetic: none -> 3.04 us  [per_device(): pair = keep + lax.ppermute(send, 'row', swap)]
  transfers between devices with their start and end apart: 0 -> 4, of which waited for: 0 -> 3; matrix products, arithmetic and copies ran while one was open for 0% -> 0% of each run, Pallas kernels for 0% -> 20%
where the time goes in v2:
time: 108 us
  Pallas kernels  45 us (42%)
  blocking collectives  39.4 us (36%)
  starting transfers between devices  11.2 us (10%)
  other arithmetic  6.18 us (6%)
  waiting for transfers between devices  4.32 us (4%)
    pallas_call x2, Pallas kernels, histogram(): pl.pallas_call(functools.partial(hist_kernel, picks), grid=(features // S...  42.7 us
    all_to_all x1, blocking collectives, per_device(): lax.all_to_all(copies, ('row', 'feat'), 0, 0, axis_index_groups=same_core...  22.2 us
    all_to_all x1, blocking collectives, per_device(): lax.all_to_all(pair, 'row', 0, 0, axis_index_groups=same_core, tiled=True)  17.2 us
    all_to_all x1, starting transfers between devices, per_device(): lax.all_to_all(pair, 'row', 0, 0, axis_index_groups=same_core, tiled=True)  5.02 us
    ppermute x2, starting transfers between devices, per_device(): pair = keep + lax.ppermute(send, 'row', swap)  4.02 us
    ppermute x2, waiting for transfers between devices, per_device(): pair = keep + lax.ppermute(send, 'row', swap)  3.49 us
    add x2, other arithmetic, per_device(): pair = keep + lax.ppermute(send, 'row', swap)  3.04 us
    pallas_call x1, Pallas kernels, gains(): pl.pallas_call(gain_kernel, out_shape=(jax.ShapeDtypeStruct((SHARE, NODES...  2.33 us
  transfers between devices with their start and end apart: 4, of which 3 were waited for; matrix products, arithmetic and copies ran while one was open for 0% of the time, Pallas kernels for 20%

profile of v2, /device:TPU:1, one launch (start us, length us, event | category | flops | bytes accessed | tf_op | source)
XLA Modules:
  0.0 107.6 jit_solution(10624297053546218894)
XLA Ops:
  0.6 0.8 fusion.1
  1.5 0.7 pad_maximum_fusion.weighted_ref
  2.2 21.3 %histogram.2 = (f32[16,2,16,256]{3,2,1,0:T(8,128)}, f32[16,2,16,256]{3,2,1,0:T(8,128)}) custom-call(s32[1]{0:T(128)} %bitcast.core_ref, s32[128,8192]{1,0:T(8,128)} %bins_ref.3, bf16[16,8192]{1,0:T(8,128)(2,1)} %pad_maximum_fusion.weighted_ref), custom_call_target="tpu_custom_call" | custom-call | flops 17179869184 | bytes 4194304 | tf_op jit(solution)/shard_map/histogram/pallas_call | solution.py:72
  23.5 3.3 %collective-permute-start = (f32[16,2,16,256]{3,2,1,0:T(8,128)}, f32[16,2,16,256]{3,2,1,0:T(8,128)S(1)}, u32[]{:S(2)}, u32[]{:S(2)}) collective-permute-start(f32[16,2,16,256]{3,2,1,0:T(8,128)} %get-tuple-element.14), channel_id=1, source_target_pairs={{0,8},{8,0},{16,24},{24,16},{32,40},{40,32},{48,56},{56,48},{64,72... | collective-permute-start | bytes 1572872 | tf_op jit(solution)/shard_map/ppermute | solution.py:154
  26.8 1.7 %collective-permute-done = f32[16,2,16,256]{3,2,1,0:T(8,128)S(1)} collective-permute-done((f32[16,2,16,256]{3,2,1,0:T(8,128)}, f32[16,2,16,256]{3,2,1,0:T(8,128)S(1)}, u32[]{:S(2)}, u32[]{:S(2)}) %collective-permute-start) | collective-permute-done | bytes 524320 | tf_op jit(solution)/shard_map/ppermute | solution.py:154
  28.5 1.9 %add.11 = f32[16,2,16,256]{3,2,1,0:T(8,128)} add(f32[16,2,16,256]{3,2,1,0:T(8,128)} %get-tuple-element.13, f32[16,2,16,256]{3,2,1,0:T(8,128)S(1)} %collective-permute-done) | non-fusion elementwise | flops 131072 | bytes 1572864 | tf_op jit(solution)/shard_map/add | solution.py:154
  30.5 5.0 %all-to-all-start = ((f32[16,2,16,256]{3,2,1,0:T(8,128)}), f32[16,2,16,256]{3,2,1,0:T(8,128)S(1)}, u32[]{:S(2)}, u32[]{:S(2)}) async-start(f32[16,2,16,256]{3,2,1,0:T(8,128)} %add.11), calls=%async_computation | async-start | bytes 1048576 | tf_op jit(solution)/shard_map/all_to_all | solution.py:156
  35.5 21.4 %histogram.3 = (f32[16,2,16,256]{3,2,1,0:T(8,128)}, f32[16,2,16,256]{3,2,1,0:T(8,128)}) custom-call(s32[1]{0:T(128)} %bitcast.core_ref, s32[128,8192]{1,0:T(8,128)} %bins_ref.3, bf16[16,8192]{1,0:T(8,128)(2,1)} %pad_maximum_fusion.weighted_ref), custom_call_target="tpu_custom_call" | custom-call | flops 17179869184 | bytes 4194304 | tf_op jit(solution)/shard_map/histogram/pallas_call | solution.py:72
  56.8 0.0 all-to-all-done
  56.8 0.0 copy-start
  56.9 0.8 collective-permute-start.1
  57.6 1.7 %collective-permute-done.1 = f32[16,2,16,256]{3,2,1,0:T(8,128)S(1)} collective-permute-done((f32[16,2,16,256]{3,2,1,0:T(8,128)}, f32[16,2,16,256]{3,2,1,0:T(8,128)S(1)}, u32[]{:S(2)}, u32[]{:S(2)}) %collective-permute-start.1) | collective-permute-done | bytes 524320 | tf_op jit(solution)/shard_map/ppermute | solution.py:154
  59.4 1.1 %add.12 = f32[16,2,16,256]{3,2,1,0:T(8,128)S(1)} add(f32[16,2,16,256]{3,2,1,0:T(8,128)} %get-tuple-element.19, f32[16,2,16,256]{3,2,1,0:T(8,128)S(1)} %collective-permute-done.1) | non-fusion elementwise | flops 131072 | bytes 1572864 | tf_op jit(solution)/shard_map/add | solution.py:154
  60.5 17.2 %all_to_all.16 = f32[16,2,16,256]{3,2,1,0:T(8,128)} all-to-all(f32[16,2,16,256]{3,2,1,0:T(8,128)S(1)} %add.12), channel_id=1, replica_groups={{0,16,32,48,64,80,96,112,128,144,160,176,192,208,224,240},{8,24,40,56,7..., dimensions={0} | all-to-all | bytes 1048576 | tf_op jit(solution)/shard_map/all_to_all | solution.py:156
  77.7 0.0 copy-done
  77.7 2.3 %gains.1 = (f32[4,8,256]{2,1,0:T(8,128)}, f32[8,128]{1,0:T(8,128)}) custom-call(f32[16,32,256]{2,1,0:T(8,128)} %bitcast.3, f32[16,32,256]{2,1,0:T(8,128)} %bitcast.4), custom_call_target="tpu_custom_call" | custom-call | tf_op jit(solution)/shard_map/gains/pallas_call | solution.py:125
  80.0 0.8 slice_reduce_fusion
  80.8 2.2 %collective-permute-start.2 = (f32[8]{0:T(128)S(1)}, f32[8]{0:T(128)S(1)}, u32[]{:S(2)}, u32[]{:S(2)}) collective-permute-start(f32[8]{0:T(128)S(1)} %slice_reduce_fusion), channel_id=1, source_target_pairs={{0,8},{8,0},{16,24},{24,16},{32,40},{40,32},{48,56},{56,48},{64,72... | collective-permute-start | bytes 104 | tf_op jit(solution)/shard_map/ppermute | solution.py:159
  83.0 0.8 collective-permute-done.2
  83.8 22.2 %all_to_all.17 = f32[128,1,8]{2,1,0:T(1,128)S(1)} all-to-all(f32[128,1,8]{2,1,0:T(1,128)S(1)} %broadcast_in_dim.33), channel_id=1, replica_groups={{0,1,2,3,4,5,6,7,16,17,18,19,20,21,22,23,32,33,34,35,36,37,38,39,48,49,..., dimensions={0} | all-to-all | bytes 8192 | tf_op jit(solution)/shard_map/all_to_all | solution.py:161
  106.0 0.2 reduce_max.9
  106.2 0.0 copy-start.1
  106.2 1.4 %broadcast_subtract_fusion = f32[4,8,256]{2,1,0:T(8,128)} fusion(f32[4,8,256]{2,1,0:T(8,128)} %get-tuple-element.22, f32[8]{0:T(128)S(1)} %reduce_max.9), kind=kLoop, calls=%fused_computation.4 | loop fusion | flops 8192 | bytes 65568 | tf_op jit(solution)/shard_map/sub | solution.py:162
  107.6 0.0 copy-done.1
  (2 shorter events, 0.0 us)
Async XLA Ops:
  23.5 5.0 %collective-permute-start = (f32[16,2,16,256]{3,2,1,0:T(8,128)}, f32[16,2,16,256]{3,2,1,0:T(8,128)S(1)}, u32[]{:S(2)}, u32[]{:S(2)}) collective-permute-start(f32[16,2,16,256]{3,2,1,0:T(8,128)} %get-tuple-element.14), channel_id=1, source_target_pairs={{0,8},{8,0},{16,24},{24,16},{32,40},{40,32},{48,56},{56,48},{64,72... | collective-permute-start | bytes 1572872 | tf_op jit(solution)/shard_map/ppermute | solution.py:154
  30.5 26.4 %all-to-all-start = ((f32[16,2,16,256]{3,2,1,0:T(8,128)}), f32[16,2,16,256]{3,2,1,0:T(8,128)S(1)}, u32[]{:S(2)}, u32[]{:S(2)}) async-start(f32[16,2,16,256]{3,2,1,0:T(8,128)} %add.11), calls=%async_computation | async-start | bytes 1048576 | tf_op jit(solution)/shard_map/all_to_all | solution.py:156
  56.8 20.8 %copy-start = (f32[16,2,16,256]{3,2,1,0:T(8,128)}, f32[16,2,16,256]{3,2,1,0:T(8,128)S(1)}, u32[]{:S(2)}) copy-start(f32[16,2,16,256]{3,2,1,0:T(8,128)S(1)} %all-to-all-done) | copy-start | bytes 1572868
  56.9 2.5 %collective-permute-start.1 = (f32[16,2,16,256]{3,2,1,0:T(8,128)}, f32[16,2,16,256]{3,2,1,0:T(8,128)S(1)}, u32[]{:S(2)}, u32[]{:S(2)}) collective-permute-start(f32[16,2,16,256]{3,2,1,0:T(8,128)} %get-tuple-element.20), channel_id=1, source_target_pairs={{0,8},{8,0},{16,24},{24,16},{32,40},{40,32},{48,56},{56,48},{64,72... | collective-permute-start | bytes 1572872 | tf_op jit(solution)/shard_map/ppermute | solution.py:154
  80.8 3.0 %collective-permute-start.2 = (f32[8]{0:T(128)S(1)}, f32[8]{0:T(128)S(1)}, u32[]{:S(2)}, u32[]{:S(2)}) collective-permute-start(f32[8]{0:T(128)S(1)} %slice_reduce_fusion), channel_id=1, source_target_pairs={{0,8},{8,0},{16,24},{24,16},{32,40},{40,32},{48,56},{56,48},{64,72... | collective-permute-start | bytes 104 | tf_op jit(solution)/shard_map/ppermute | solution.py:159
  106.2 1.5 %copy-start.1 = (f32[8]{0:T(128)}, f32[8]{0:T(128)S(1)}, u32[]{:S(2)}) copy-start(f32[8]{0:T(128)S(1)} %reduce_max.9) | copy-start | bytes 100

commit v3 on v2

--- a/solution.py
+++ b/solution.py
@@ -17,7 +17,7 @@
 CHUNK = 512
 SHARE = 4
 CORES = 2
-PIECES = ((0, 1), (2, 3))
+PIECES = ((0, 1, 2, 3),)
 
 
 def hist_kernel(picks, core_ref, bins_ref, weighted_ref, keep_ref, send_ref, held_ref):
@@ -80,7 +80,7 @@
         out_specs=[pl.BlockSpec((step, count, STATS, BINS), lambda i: (i, 0, 0, 0))] * 2,
         out_shape=[jax.ShapeDtypeStruct((chips, count, STATS, BINS), jnp.float32)] * 2,
         scratch_shapes=[pltpu.VMEM((SUB // SHARE, count, STATS, BINS), jnp.float32)],
-        compiler_params=pltpu.CompilerParams(vmem_limit_bytes=60 * 2**20),
+        compiler_params=pltpu.CompilerParams(vmem_limit_bytes=48 * 2**20),
         cost_estimate=pl.CostEstimate(
             flops=2 * features * count // SHARE * rows * LOW * BINS,
             bytes_accessed=4 * features * rows,
@@ -128,7 +128,7 @@
             jax.ShapeDtypeStruct((SHARE, NODES, BINS), jnp.float32),
             jax.ShapeDtypeStruct((NODES, 128), jnp.float32),
         ),
-        compiler_params=pltpu.CompilerParams(vmem_limit_bytes=60 * 2**20),
+        compiler_params=pltpu.CompilerParams(vmem_limit_bytes=48 * 2**20),
         name="gains",
     )(*parts)
 
@@ -139,7 +139,6 @@
     chips = row_size // CORES
     swap = [(i, i ^ 1) for i in range(row_size)]
     same_core = [[chip * CORES + c for chip in range(chips)] for c in range(CORES)]
-    same_core_all = [[i * feat_size + z for i in group for z in range(feat_size)] for group in same_core]
     member = node[None, :] == jnp.arange(NODES, dtype=jnp.int32)[:, None]
     zero = jnp.zeros((), jnp.bfloat16)
     weighted = jnp.concatenate(
@@ -149,16 +148,12 @@
     parts = []
     for picks in PIECES:
         keep, send = histogram(bins, weighted, core, picks)
-        if parts:
-            send, parts[-1] = lax.optimization_barrier((send, parts[-1]))
         pair = keep + lax.ppermute(send, "row", swap)
-        pair, weighted = lax.optimization_barrier((pair, weighted))
         parts.append(lax.all_to_all(pair, "row", 0, 0, axis_index_groups=same_core, tiled=True))
     gain, own_best = gains(*parts)
     own_best = own_best[:, 0]
-    own_best = jnp.maximum(own_best, lax.ppermute(own_best, "row", swap))
-    copies = jnp.broadcast_to(own_best, (chips * feat_size, NODES))
-    best = jnp.max(lax.all_to_all(copies, ("row", "feat"), 0, 0, axis_index_groups=same_core_all, tiled=True), axis=0)
+    copies = jnp.broadcast_to(own_best, (row_size * feat_size, NODES))
+    best = jnp.max(lax.all_to_all(copies, ("row", "feat"), 0, 0, tiled=True), axis=0)
     return (gain - best[None, :, None], best)
 
 

time: 108 us -> 93.4 us (0.86)
  starting transfers between devices: 11.2 us -> 3.33 us
  blocking collectives: 39.4 us -> 46.3 us
  Pallas kernels: 45 us -> 38.3 us
  other arithmetic: 6.18 us -> 2.03 us
  waiting for transfers between devices: 4.32 us -> 2.29 us
    all_to_all x1 -> x0, starting transfers between devices: 5.02 us -> none  [per_device(): lax.all_to_all(pair, 'row', 0, 0, axis_index_groups=same_core, tiled=True)]
    pallas_call x2 -> x1, Pallas kernels: 42.7 us -> 37.8 us  [histogram(): pl.pallas_call(functools.partial(hist_kernel, picks), grid=(features // S...]
    all_to_all x1, blocking collectives: 17.2 us -> 20.8 us  [per_device(): lax.all_to_all(pair, 'row', 0, 0, axis_index_groups=same_core, tiled=True)]
    all_to_all x1, blocking collectives: 22.2 us -> 25.5 us  [per_device(): lax.all_to_all(copies, ('row', 'feat'), 0, 0, tiled=True)]
    add x2 -> x1, other arithmetic: 3.04 us -> 0.21 us  [per_device(): pair = keep + lax.ppermute(send, 'row', swap)]
    ppermute x1 -> x0, starting transfers between devices: 2.17 us -> none  [per_device(): own_best = jnp.maximum(own_best, lax.ppermute(own_best, 'row', swap))]
    pallas_call x1, Pallas kernels: 2.33 us -> 0.42 us  [gains(): pl.pallas_call(gain_kernel, out_shape=(jax.ShapeDtypeStruct((SHARE, NODES...]
    ppermute x2 -> x1, waiting for transfers between devices: 3.49 us -> 2.29 us  [per_device(): pair = keep + lax.ppermute(send, 'row', swap)]
  transfers between devices with their start and end apart: 4 -> 1, of which waited for: 3 -> 1; matrix products, arithmetic and copies ran while one was open for 0% -> 0% of each run, Pallas kernels for 20% -> 0%
where the time goes in v3:
time: 93.4 us; the launch traced here: 93.1 us
  blocking collectives  46.3 us (50%)
  Pallas kernels  38.3 us (41%)
  starting transfers between devices  3.33 us (4%)
  waiting for transfers between devices  2.29 us (2%)
  other arithmetic  2.03 us (2%)
    pallas_call x1, Pallas kernels, histogram(): pl.pallas_call(functools.partial(hist_kernel, picks), grid=(features // S...  37.8 us
    all_to_all x1, blocking collectives, per_device(): lax.all_to_all(copies, ('row', 'feat'), 0, 0, tiled=True)  25.5 us
    all_to_all x1, blocking collectives, per_device(): lax.all_to_all(pair, 'row', 0, 0, axis_index_groups=same_core, tiled=True)  20.8 us
    ppermute x1, starting transfers between devices, per_device(): pair = keep + lax.ppermute(send, 'row', swap)  3.33 us
    ppermute x1, waiting for transfers between devices, per_device(): pair = keep + lax.ppermute(send, 'row', swap)  2.29 us
  transfers between devices with their start and end apart: 1, of which 1 were waited for; matrix products, arithmetic and copies ran while one was open for 0% of the time, Pallas kernels for 0%

profile of v3, /device:TPU:1, one launch (start us, length us, event | category | flops | bytes accessed | tf_op | source)
XLA Modules:
  0.0 93.1 jit_solution(2946531088700422980)
XLA Ops:
  0.6 0.8 fusion.1
  1.5 37.8 %histogram.1 = (f32[16,4,16,256]{3,2,1,0:T(8,128)S(1)}, f32[16,4,16,256]{3,2,1,0:T(8,128)S(1)}) custom-call(s32[1]{0:T(128)} %bitcast.core_ref, s32[128,8192]{1,0:T(8,128)} %bins_ref.1, bf16[16,8192]{1,0:T(8,128)(2,1)S(1)} %pad_maximum_fusion.weighted_ref), custom_call_target="tpu_custom_call" | custom-call | flops 34359738368 | bytes 4194304 | tf_op jit(solution)/shard_map/histogram/pallas_call | solution.py:72
  39.4 3.3 %collective-permute-start = (f32[16,4,16,256]{3,2,1,0:T(8,128)S(1)}, f32[16,4,16,256]{3,2,1,0:T(8,128)S(1)}, u32[]{:S(2)}, u32[]{:S(2)}) collective-permute-start(f32[16,4,16,256]{3,2,1,0:T(8,128)S(1)} %get-tuple-element.7), channel_id=1, source_target_pairs={{0,8},{8,0},{16,24},{24,16},{32,40},{40,32},{48,56},{56,48},{64,72... | collective-permute-start | bytes 3145736 | tf_op jit(solution)/shard_map/ppermute | solution.py:151
  42.7 2.3 %collective-permute-done = f32[16,4,16,256]{3,2,1,0:T(8,128)S(1)} collective-permute-done((f32[16,4,16,256]{3,2,1,0:T(8,128)S(1)}, f32[16,4,16,256]{3,2,1,0:T(8,128)S(1)}, u32[]{:S(2)}, u32[]{:S(2)}) %collective-permute-start) | collective-permute-done | bytes 1048608 | tf_op jit(solution)/shard_map/ppermute | solution.py:151
  45.0 0.2 add.8
  45.2 20.8 %all_to_all.11 = f32[16,4,16,256]{3,2,1,0:T(8,128)S(1)} all-to-all(f32[16,4,16,256]{3,2,1,0:T(8,128)S(1)} %add.8), channel_id=1, replica_groups={{0,16,32,48,64,80,96,112,128,144,160,176,192,208,224,240},{8,24,40,56,7..., dimensions={0} | all-to-all | bytes 2097152 | tf_op jit(solution)/shard_map/all_to_all | solution.py:152
  66.0 0.4 gains.1
  66.4 0.1 slice_reduce_fusion
  66.5 0.1 broadcast_in_dim.36
  66.6 25.5 %all_to_all.12 = f32[256,1,8]{2,1,0:T(1,128)S(1)} all-to-all(f32[256,1,8]{2,1,0:T(1,128)S(1)} %broadcast_in_dim.36), channel_id=1, replica_groups=mesh['row'=32,'feat'=8] {'row','feat'}, dimensions={0} | all-to-all | bytes 16384 | tf_op jit(solution)/shard_map/all_to_all | solution.py:156
  92.1 0.3 reduce_max.9
  92.4 0.0 copy-start
  92.4 0.7 broadcast_subtract_fusion
  93.1 0.0 copy-done
  (1 shorter events, 0.0 us)
Async XLA Ops:
  39.4 5.6 %collective-permute-start = (f32[16,4,16,256]{3,2,1,0:T(8,128)S(1)}, f32[16,4,16,256]{3,2,1,0:T(8,128)S(1)}, u32[]{:S(2)}, u32[]{:S(2)}) collective-permute-start(f32[16,4,16,256]{3,2,1,0:T(8,128)S(1)} %get-tuple-element.7), channel_id=1, source_target_pairs={{0,8},{8,0},{16,24},{24,16},{32,40},{40,32},{48,56},{56,48},{64,72... | collective-permute-start | bytes 3145736 | tf_op jit(solution)/shard_map/ppermute | solution.py:151
  92.4 0.7 copy-start

commit v4 on v0

v4 whole, which is shorter than its diff:
```python
import functools

import jax
import jax.numpy as jnp
from jax import lax
from jax.experimental import pallas as pl
from jax.experimental.pallas import tpu as pltpu
from jax.sharding import PartitionSpec as P

BINS = 256
NODES = 8
LANES = 128
CHUNK = 256
LOW = 16
HIGH = BINS // LOW
CORES = 2
SHARE = 4
BYTES = 4
TILES = 16
BOTH = 2 * HIGH


def iota(shape, dim):
    return lax.broadcasted_iota(jnp.int32, shape, dim)


def ones_where(condition, dtype=jnp.float32):
    return jnp.where(condition, 1.0, 0.0).astype(dtype)


def exact_dot(a, b):
    return jnp.dot(a, b, preferred_element_type=jnp.float32, precision=lax.Precision.HIGHEST)


def dot_t(a, b):
    return lax.dot_general(a, b, (((1,), (1,)), ((), ())), preferred_element_type=jnp.float32)


def plan_kernel(node_ref, table_ref, order_ref):
    tiles = node_ref.shape[0]
    node = node_ref[...]
    members = [node == n for n in range(NODES)]
    stacked = jnp.concatenate([ones_where(m) for m in members], 0).astype(jnp.bfloat16)
    before = ones_where(iota((LANES, LANES), 0) < iota((LANES, LANES), 1), jnp.bfloat16)
    ranks = jnp.dot(stacked, before, preferred_element_type=jnp.float32)
    place = jnp.zeros((tiles, LANES), jnp.float32)
    first = jnp.zeros((tiles, 1), jnp.float32)
    counts = jnp.zeros((NODES, tiles), jnp.float32)
    for n in range(NODES):
        at = slice(n * tiles, (n + 1) * tiles)
        place = place + jnp.where(members[n], ranks[at] + first, 0.0)
        first = first + jnp.sum(ones_where(members[n]), axis=1, keepdims=True)
        counts = counts + dot_t(ones_where(iota((NODES, LANES), 0) == n, jnp.bfloat16), stacked[at])
    earlier = exact_dot(counts, ones_where(iota((tiles, tiles), 0) < iota((tiles, tiles), 1)))
    lower = ones_where(iota((NODES, NODES), 0) > iota((NODES, NODES), 1))
    start = exact_dot(lower, counts)
    total = jnp.sum(counts, axis=1, keepdims=True).astype(jnp.int32)
    padded = ((total + (CHUNK - 1)) // CHUNK * CHUNK).astype(jnp.float32)
    base = exact_dot(lower, jnp.broadcast_to(padded, (NODES, LANES)))
    ended = ones_where(base + padded <= (iota((NODES, LANES), 1) * CHUNK).astype(jnp.float32))
    owner = jnp.minimum(jnp.sum(ended, axis=0, keepdims=True), NODES - 1.0)
    table_ref[0:NODES, :tiles] = (base[:, :tiles] + earlier).astype(jnp.int32)
    table_ref[NODES : 2 * NODES, :tiles] = counts.astype(jnp.int32)
    table_ref[2 * NODES : 3 * NODES, :tiles] = start.astype(jnp.int32)
    table_ref[3 * NODES : 4 * NODES, :] = jnp.broadcast_to(owner, (NODES, LANES)).astype(jnp.int32)
    lane = iota((8, LANES), 1).astype(jnp.bfloat16)
    slot = iota((LANES, LANES), 0).astype(jnp.float32)
    for t in range(tiles):
        hit = ones_where(jnp.broadcast_to(place[t : t + 1], (LANES, LANES)) == slot, jnp.bfloat16)
        order_ref[t] = dot_t(lane, hit).astype(jnp.int32)


def plan(node):
    tiles = node.shape[0] // LANES
    return pl.pallas_call(
        plan_kernel,
        out_shape=(
            jax.ShapeDtypeStruct((4 * NODES, LANES), jnp.int32),
            jax.ShapeDtypeStruct((tiles, 8, LANES), jnp.int32),
        ),
        compiler_params=pltpu.CompilerParams(vmem_limit_bytes=16 * 2**20),
        name="plan",
    )(node.reshape(tiles, LANES))


def place_kernel(table_ref, bins_ref, grads_ref, hess_ref, order_ref, packed_ref, stats_ref):
    step = pl.program_id(0)

    @pl.when(step == 0)
    def _():
        stats_ref[...] = jnp.zeros_like(stats_ref)

    lane = iota((8, LANES), 1)
    top = iota((8, LANES), 0) == 0
    groups = packed_ref.shape[1] // 8
    for i in range(TILES):
        at = slice(i * LANES, (i + 1) * LANES)
        t = step * TILES + i
        values = []
        for g in range(groups):
            word = bins_ref[8 * g : 8 * g + 8, at]
            for k in range(1, BYTES):
                first = 8 * (g + groups * k)
                word = word | (bins_ref[first : first + 8, at] << (8 * k))
            values.append(word)
        grad = jnp.broadcast_to(grads_ref[:, at].astype(jnp.float32), (8, LANES))
        hess = jnp.broadcast_to(hess_ref[:, at].astype(jnp.float32), (8, LANES))
        values.append(jnp.where(top, grad, hess))
        order = order_ref[i]
        values = [jnp.take_along_axis(v, order, axis=1) for v in values]
        for n in range(NODES):
            dest = table_ref[n, t]
            count = table_ref[NODES + n, t]
            start = table_ref[2 * NODES + n, t]
            tile = dest >> 7
            off = dest & (LANES - 1)
            inside = ((lane - off) & (LANES - 1)) < count
            here = inside & (lane >= off)
            beyond = inside & (lane < off)
            for g, value in enumerate(values):
                moved = pltpu.roll(value, (off - start) & (LANES - 1), axis=1)
                ref, rows = (packed_ref, slice(8 * g, 8 * g + 8)) if g < groups else (stats_ref, slice(0, 8))
                pltpu.store(ref.at[tile, rows], moved, mask=here)
                pltpu.store(ref.at[tile + 1, rows], moved, mask=beyond)


def place(table, order, bins, grads, hess):
    features, rows = bins.shape
    tiles = rows // LANES
    room = tiles + 2 * NODES
    words = features // BYTES
    width = TILES * LANES
    return pl.pallas_call(
        place_kernel,
        grid=(tiles // TILES,),
        in_specs=[
            pl.BlockSpec(memory_space=pltpu.SMEM),
            pl.BlockSpec((features, width), lambda i: (0, i)),
            pl.BlockSpec((1, width), lambda i: (0, i)),
            pl.BlockSpec((1, width), lambda i: (0, i)),
            pl.BlockSpec((TILES, 8, LANES), lambda i: (i, 0, 0)),
        ],
        out_specs=[
            pl.BlockSpec((room, words, LANES), lambda i: (0, 0, 0)),
            pl.BlockSpec((room, 8, LANES), lambda i: (0, 0, 0)),
        ],
        out_shape=[
            jax.ShapeDtypeStruct((room, words, LANES), jnp.int32),
            jax.ShapeDtypeStruct((room, 8, LANES), jnp.float32),
        ],
        compiler_params=pltpu.CompilerParams(vmem_limit_bytes=50 * 2**20),
        name="place",
    )(table, bins, grads[None], hess[None], order)


def hist_kernel(chunks, per_step, core_ref, table_ref, packed_ref, stats_ref, keep_ref, send_ref, spread_ref, sums_ref):
    core = core_ref[0]
    level = iota((HIGH, CHUNK), 0).astype(jnp.bfloat16)
    zero = jnp.zeros((), jnp.bfloat16)
    one = jnp.ones((), jnp.bfloat16)
    lane_group = iota((BOTH, LANES), 1) // LOW

    @pl.when((pl.program_id(0) == 0) & (pl.program_id(1) == 0))
    def _():
        for c in range(chunks):
            for half in range(CHUNK // LANES):
                for s in range(2):
                    row = stats_ref[2 * c + half, s : s + 1, :].astype(jnp.bfloat16)
                    spread_ref[c, HIGH * s : HIGH * (s + 1), half * LANES : (half + 1) * LANES] = jnp.broadcast_to(
                        row, (HIGH, LANES)
                    )

    sums_ref[...] = jnp.zeros_like(sums_ref)
    for c in range(chunks):
        raw = jnp.concatenate([packed_ref[2 * c], packed_ref[2 * c + 1]], axis=1)
        grad = spread_ref[c, 0:HIGH]
        hess = spread_ref[c, HIGH:BOTH]
        n = table_ref[3 * NODES, c]
        for q in range(per_step):
            words = raw >> ((pl.program_id(1) * per_step + q) * 8)
            low = (words & (LOW - 1)).astype(jnp.bfloat16)
            high = ((words >> 4) & (HIGH - 1)).astype(jnp.bfloat16)
            left = []
            right = []
            for j in range(8):
                hit = jnp.broadcast_to(high[j : j + 1], (HIGH, CHUNK)) == level
                left.append(jnp.where(hit, grad, zero))
                left.append(jnp.where(hit, hess, zero))
                right.append(jnp.where(jnp.broadcast_to(low[j : j + 1], (LOW, CHUNK)) == level, one, zero))
            product = dot_t(jnp.concatenate(left, 0), jnp.concatenate(right, 0))
            own = product[0:BOTH]
            for j in range(1, 8):
                own = jnp.where(lane_group == j, product[BOTH * j : BOTH * (j + 1)], own)
            sums_ref[q, n] = sums_ref[q, n] + own
    half = LANES // 2
    for q in range(per_step):
        for pair in range(NODES // 2):
            even = sums_ref[q, 2 * pair]
            odd = sums_ref[q, 2 * pair + 1]
            first = jnp.concatenate([even[:, :half], odd[:, :half]], axis=1)
            second = jnp.concatenate([even[:, half:], odd[:, half:]], axis=1)
            keep_ref[q, 0, pair] = jnp.where(core == 0, first, second)
            send_ref[q, 0, pair] = jnp.where(core == 0, second, first)


def histogram(core, table, packed, stats, rows, per_step=4):
    room, words, _ = packed.shape
    blocks = words // 8
    chunks = rows // CHUNK + NODES - 1
    out = jax.ShapeDtypeStruct((BYTES, blocks, NODES // 2, BOTH, LANES), jnp.float32)
    keep, send = pl.pallas_call(
        functools.partial(hist_kernel, chunks, per_step),
        grid=(blocks, BYTES // per_step),
        in_specs=[
            pl.BlockSpec(memory_space=pltpu.SMEM),
            pl.BlockSpec(memory_space=pltpu.SMEM),
            pl.BlockSpec((room, 8, LANES), lambda i, k: (0, i, 0)),
            pl.BlockSpec((room, 8, LANES), lambda i, k: (0, 0, 0)),
        ],
        out_specs=[pl.BlockSpec((per_step, 1, NODES // 2, BOTH, LANES), lambda i, k: (k, i, 0, 0, 0))] * 2,
        out_shape=[out, out],
        scratch_shapes=[
            pltpu.VMEM((chunks, BOTH, CHUNK), jnp.bfloat16),
            pltpu.VMEM((per_step, NODES, BOTH, LANES), jnp.float32),
        ],
        compiler_params=pltpu.CompilerParams(vmem_limit_bytes=32 * 2**20),
        name="histogram",
    )(core, table, packed, stats)
    return [v.reshape(BYTES * blocks, NODES // 2, BOTH, LANES) for v in (keep, send)]


def gain_kernel(parts_ref, gain_ref, best_ref):
    hist = parts_ref[0]
    for i in range(1, parts_ref.shape[0]):
        hist = hist + parts_ref[i]
    rows = hist.shape[0]
    row_a, row_b = iota((rows, rows), 0), iota((rows, rows), 1)
    lane_a, lane_b = iota((LANES, LANES), 0), iota((LANES, LANES), 1)
    same_lows = lane_a // LOW == lane_b // LOW
    same_highs = row_a // HIGH == row_b // HIGH
    within = exact_dot(hist, ones_where(same_lows & (lane_a <= lane_b)))
    summed = exact_dot(hist, ones_where(same_lows))
    left = within + exact_dot(ones_where(same_highs & (row_a > row_b)), summed)
    total = exact_dot(ones_where(same_highs), summed)
    left = left.reshape(NODES // 2, 2, HIGH, LANES)
    total = total.reshape(NODES // 2, 2, HIGH, LANES)
    grad_left, hess_left = left[:, 0], left[:, 1]
    grad_total, hess_total = total[:, 0], total[:, 1]
    gain = grad_left * grad_left / (hess_left + 1.0)
    gain = gain + (grad_total - grad_left) ** 2 / (hess_total - hess_left + 1.0)
    gain = gain - grad_total * grad_total / (hess_total + 1.0)
    most = jnp.max(gain, axis=1)
    half = LANES // 2
    for odd in range(2):
        best = jnp.max(most[:, odd * half : (odd + 1) * half], axis=1, keepdims=True)
        for pair in range(NODES // 2):
            best_ref[2 * pair + odd] = jnp.broadcast_to(best[pair], (LANES,))
    gain = gain.reshape(NODES // 2 * HIGH, LANES)
    from_lane, to_bin = iota((LANES, BINS), 0), iota((LANES, BINS), 1)
    own_high = iota((NODES // 2 * HIGH, BINS), 0) % HIGH == iota((NODES // 2 * HIGH, BINS), 1) // LOW
    for odd in range(2):
        for slot in range(SHARE):
            take = ones_where(from_lane == (odd * SHARE + slot) * LOW + to_bin % LOW)
            spread = jnp.where(own_high, exact_dot(gain, take), 0.0)
            rows_out = jnp.sum(spread.reshape(NODES // 2, HIGH, BINS), axis=1)
            for pair in range(NODES // 2):
                gain_ref[slot, 2 * pair + odd] = rows_out[pair]


def gains(parts):
    chips = parts.shape[0]
    return pl.pallas_call(
        gain_kernel,
        out_shape=(
            jax.ShapeDtypeStruct((SHARE, NODES, BINS), jnp.float32),
            jax.ShapeDtypeStruct((NODES, LANES), jnp.float32),
        ),
        compiler_params=pltpu.CompilerParams(vmem_limit_bytes=32 * 2**20),
        name="gains",
    )(parts.reshape(chips, NODES // 2 * BOTH, LANES))


def per_device(bins, grads, hess, node):
    row_size = lax.axis_size("row")
    feat_size = lax.axis_size("feat")
    swap = [(i, i ^ 1) for i in range(row_size)]
    same_core = [[chip * CORES + c for chip in range(row_size // CORES)] for c in range(CORES)]
    core = (lax.axis_index("row") % CORES)[None]
    table, order = plan(node)
    packed, stats = place(table, order, bins, grads, hess)
    keep, send = histogram(core, table, packed, stats, bins.shape[1])
    pair = keep + lax.ppermute(send, "row", swap)
    gain, own_best = gains(lax.all_to_all(pair, "row", 0, 0, axis_index_groups=same_core, tiled=True))
    copies = jnp.broadcast_to(own_best[:, 0], (row_size * feat_size, NODES))
    best = jnp.max(lax.all_to_all(copies, ("row", "feat"), 0, 0, tiled=True), axis=0)
    return (gain - best[None, :, None], best)


def solution(mesh):
    return jax.shard_map(
        per_device,
        mesh=mesh,
        in_specs=(P("feat", "row"), P("row"), P("row"), P("row")),
        out_specs=(P(("feat", "row"), None, None), P()),
        check_vma=False,
    )
```

time: 434 us -> 91.8 us (0.21)
  matrix products: 200 us -> 0 us
  blocking collectives: 143 us -> 46.3 us
  waiting for transfers between devices: 55.6 us -> 2.29 us
  Pallas kernels: 0 us -> 35.2 us
  local copies, waits for them, and re-layouts: 16.5 us -> 2.42 us
  between operations: 14.1 us -> 0.69 us
    dot_general x16 -> x0, matrix products: 200 us -> none  [block_hist(): jnp.einsum('kr,frb->fkb', weighted, onehot, preferred_element_type=jnp.fl...]
    pmax x1 -> x0, blocking collectives: 77 us -> none  [per_device(): best = lax.pmax(local_best, ('row', 'feat'))]
    psum x1 -> x0, blocking collectives: 65.6 us -> none  [per_device(): node_sums = lax.psum(own_sums, 'row')]
    psum x1 -> x0, waiting for transfers between devices: 55.6 us -> none  [per_device(): summed = lax.psum(partial_hist, 'row')]
    all_to_all x0 -> x2, blocking collectives: none -> 46.3 us  [the longest x1 25.5 us: per_device(): lax.all_to_all(copies, ('row', 'feat'), 0, 0, tiled=True)]
    pallas_call x0 -> x4, Pallas kernels: none -> 35.2 us  [the longest x1 24.1 us: histogram(): pl.pallas_call(functools.partial(hist_kernel, chunks, per_step), grid=(bl...]
    eq x16 -> x0, local copies, waits for them, and re-layouts: 15.5 us -> none  [block_hist(): onehot = (columns[:, :, None] == levels[None, None, :]).astype(jnp.bfloat16)]
where the time goes in v4:
time: 91.8 us; the launch traced here: 91.4 us
  blocking collectives  46.3 us (50%)
  Pallas kernels  35.2 us (38%)
  starting transfers between devices  3.33 us (4%)
  local copies, waits for them, and re-layouts  2.42 us (3%)
  waiting for transfers between devices  2.29 us (2%)
  other arithmetic  1.2 us (1%)
    all_to_all x1, blocking collectives, per_device(): lax.all_to_all(copies, ('row', 'feat'), 0, 0, tiled=True)  25.5 us
    pallas_call x1, Pallas kernels, histogram(): pl.pallas_call(functools.partial(hist_kernel, chunks, per_step), grid=(bl...  24.1 us
    all_to_all x1, blocking collectives, per_device(): lax.all_to_all(pair, 'row', 0, 0, axis_index_groups=same_core, tiled=True)  20.8 us
    pallas_call x1, Pallas kernels, place(): pl.pallas_call(place_kernel, grid=(tiles // TILES,), in_specs=[pl.BlockSp...  8.36 us
    ppermute x1, starting transfers between devices, per_device(): pair = keep + lax.ppermute(send, 'row', swap)  3.33 us
    ppermute x1, waiting for transfers between devices, per_device(): pair = keep + lax.ppermute(send, 'row', swap)  2.29 us
  transfers between devices with their start and end apart: 1, of which 1 were waited for; matrix products, arithmetic and copies ran while one was open for 0% of the time, Pallas kernels for 0%

profile of v4, /device:TPU:1, one launch (start us, length us, event | category | flops | bytes accessed | tf_op | source)
XLA Modules:
  0.0 91.4 jit_solution(6281914044526059498)
XLA Ops:
  0.6 0.7 broadcast_in_dim.16.grads_ref
  1.4 0.7 broadcast_in_dim.17.hess_ref
  2.1 0.0 copy-start
  2.1 0.7 copy-done
  2.9 1.5 %plan.1 = (s32[32,128]{1,0:T(8,128)S(1)}, s32[64,8,128]{2,1,0:T(8,128)S(1)}) custom-call(s32[64,128]{1,0:T(8,128)S(1)} %bitcast.7), custom_call_target="tpu_custom_call" | custom-call | tf_op jit(solution)/shard_map/plan/pallas_call | solution.py:75
  4.4 8.4 %place.1 = (s32[80,32,128]{2,1,0:T(8,128)S(1)}, f32[80,8,128]{2,1,0:T(8,128)S(1)}) custom-call(s32[32,128]{1,0:T(8,128)S(1)} %get-tuple-element.10.table_ref, s32[128,8192]{1,0:T(8,128)} %bins_ref.1, bf16[1,8192]{1,0:T(2,128)(2,1)S(1)} %broadcast_in_dim.16.grads_ref, bf16[1,8192]{1,0:T(2,128)(2,1)S(1)} %broadcast_in_dim.17.hess_ref, ...), custom_call_target="tpu_custom_call" | custom-call | tf_op jit(solution)/shard_map/place/pallas_call | solution.py:133
  12.8 24.1 %histogram.1 = (f32[4,4,4,32,128]{4,3,2,1,0:T(8,128)S(1)}, f32[4,4,4,32,128]{4,3,2,1,0:T(8,128)S(1)}) custom-call(s32[1]{0:T(128)} %bitcast.core_ref, s32[32,128]{1,0:T(8,128)S(1)} %get-tuple-element.10.table_ref, s32[80,32,128]{2,1,0:T(8,128)S(1)} %get-tuple-element.12.packed_ref, f32[80,8,128]{2,1,0:T(8,128)S(1)} %get-tuple-element.13.stats_ref), custom_call_target="tpu_custom_call" | custom-call | tf_op jit(solution)/shard_map/histogram/pallas_call | solution.py:211
  36.9 3.3 %collective-permute-start = (f32[16,4,32,128]{3,2,1,0:T(8,128)S(1)}, f32[16,4,32,128]{3,2,1,0:T(8,128)S(1)}, u32[]{:S(2)}, u32[]{:S(2)}) collective-permute-start(f32[16,4,32,128]{3,2,1,0:T(8,128)S(1)} %bitcast.8), channel_id=1, source_target_pairs={{0,8},{8,0},{16,24},{24,16},{32,40},{40,32},{48,56},{56,48},{64,72... | collective-permute-start | bytes 3145736 | tf_op jit(solution)/shard_map/ppermute | solution.py:292
  40.3 2.3 %collective-permute-done = f32[16,4,32,128]{3,2,1,0:T(8,128)S(1)} collective-permute-done((f32[16,4,32,128]{3,2,1,0:T(8,128)S(1)}, f32[16,4,32,128]{3,2,1,0:T(8,128)S(1)}, u32[]{:S(2)}, u32[]{:S(2)}) %collective-permute-start) | collective-permute-done | bytes 1048608 | tf_op jit(solution)/shard_map/ppermute | solution.py:292
  42.6 0.2 bitcast_add_fusion
  42.8 20.8 %all_to_all.11 = f32[16,4,32,128]{3,2,1,0:T(8,128)S(1)} all-to-all(f32[16,4,32,128]{3,2,1,0:T(8,128)S(1)} %bitcast_add_fusion), channel_id=1, replica_groups={{0,16,32,48,64,80,96,112,128,144,160,176,192,208,224,240},{8,24,40,56,7..., dimensions={0} | all-to-all | bytes 2097152 | tf_op jit(solution)/shard_map/all_to_all | solution.py:293
  63.6 1.2 %gains.1 = (f32[4,8,256]{2,1,0:T(8,128)S(1)}, f32[8,128]{1,0:T(8,128)S(1)}) custom-call(f32[16,128,128]{2,1,0:T(8,128)S(1)} %bitcast.6), custom_call_target="tpu_custom_call" | custom-call | tf_op jit(solution)/shard_map/gains/pallas_call | solution.py:272
  64.8 0.1 slice_reduce_fusion
  64.9 0.1 broadcast_in_dim.19
  65.0 25.5 %all_to_all.12 = f32[256,1,8]{2,1,0:T(1,128)S(1)} all-to-all(f32[256,1,8]{2,1,0:T(1,128)S(1)} %broadcast_in_dim.19), channel_id=1, replica_groups=mesh['row'=32,'feat'=8] {'row','feat'}, dimensions={0} | all-to-all | bytes 16384 | tf_op jit(solution)/shard_map/all_to_all | solution.py:295
  90.5 0.3 reduce_max.9
  90.7 0.0 copy-start.1
  90.7 0.7 broadcast_subtract_fusion
  91.4 0.0 copy-done.1
Async XLA Ops:
  2.1 0.8 copy-start
  36.9 5.6 %collective-permute-start = (f32[16,4,32,128]{3,2,1,0:T(8,128)S(1)}, f32[16,4,32,128]{3,2,1,0:T(8,128)S(1)}, u32[]{:S(2)}, u32[]{:S(2)}) collective-permute-start(f32[16,4,32,128]{3,2,1,0:T(8,128)S(1)} %bitcast.8), channel_id=1, source_target_pairs={{0,8},{8,0},{16,24},{24,16},{32,40},{40,32},{48,56},{56,48},{64,72... | collective-permute-start | bytes 3145736 | tf_op jit(solution)/shard_map/ppermute | solution.py:292
  90.7 0.7 copy-start.1

commit v5 on v4

--- a/solution.py
+++ b/solution.py
@@ -17,6 +17,8 @@
 SHARE = 4
 BYTES = 4
 TILES = 16
+OWNER = 3 * NODES
+LIMIT = OWNER + 1
 BOTH = 2 * HIGH
 
 
@@ -28,6 +30,10 @@
     return jnp.where(condition, 1.0, 0.0).astype(dtype)
 
 
+def tiled(row):
+    return pltpu.with_memory_space_constraint(row.reshape(row.shape[0] // LANES, LANES), pltpu.HBM)
+
+
 def exact_dot(a, b):
     return jnp.dot(a, b, preferred_element_type=jnp.float32, precision=lax.Precision.HIGHEST)
 
@@ -36,7 +42,26 @@
     return lax.dot_general(a, b, (((1,), (1,)), ((), ())), preferred_element_type=jnp.float32)
 
 
-def plan_kernel(node_ref, table_ref, order_ref):
+def three(x):
+    first = x.astype(jnp.bfloat16)
+    rest = x - first.astype(jnp.float32)
+    second = rest.astype(jnp.bfloat16)
+    return [first, second, (rest - second.astype(jnp.float32)).astype(jnp.bfloat16)]
+
+
+def times_ones(x, ones):
+    rows = x.shape[0]
+    parts = jnp.dot(jnp.concatenate(three(x), 0), ones, preferred_element_type=jnp.float32)
+    return parts[:rows] + parts[rows : 2 * rows] + parts[2 * rows :]
+
+
+def ones_times(ones, x):
+    lanes = x.shape[1]
+    parts = jnp.dot(ones, jnp.concatenate(three(x), 1), preferred_element_type=jnp.float32)
+    return parts[:, :lanes] + parts[:, lanes : 2 * lanes] + parts[:, 2 * lanes :]
+
+
+def write_plan(node_ref, table_ref, order_ref):
     tiles = node_ref.shape[0]
     node = node_ref[...]
     members = [node == n for n in range(NODES)]
@@ -57,12 +82,15 @@
     total = jnp.sum(counts, axis=1, keepdims=True).astype(jnp.int32)
     padded = ((total + (CHUNK - 1)) // CHUNK * CHUNK).astype(jnp.float32)
     base = exact_dot(lower, jnp.broadcast_to(padded, (NODES, LANES)))
-    ended = ones_where(base + padded <= (iota((NODES, LANES), 1) * CHUNK).astype(jnp.float32))
-    owner = jnp.minimum(jnp.sum(ended, axis=0, keepdims=True), NODES - 1.0)
+    at_chunk = (iota((NODES, LANES), 1) * CHUNK).astype(jnp.float32)
+    holds = ones_where((base <= at_chunk) & (at_chunk < base + padded))
+    owner = jnp.sum(holds * iota((NODES, LANES), 0).astype(jnp.float32), axis=0, keepdims=True)
+    limit = jnp.sum(holds * (base + total.astype(jnp.float32)), axis=0, keepdims=True)
     table_ref[0:NODES, :tiles] = (base[:, :tiles] + earlier).astype(jnp.int32)
     table_ref[NODES : 2 * NODES, :tiles] = counts.astype(jnp.int32)
     table_ref[2 * NODES : 3 * NODES, :tiles] = start.astype(jnp.int32)
-    table_ref[3 * NODES : 4 * NODES, :] = jnp.broadcast_to(owner, (NODES, LANES)).astype(jnp.int32)
+    table_ref[OWNER : OWNER + 1, :] = owner.astype(jnp.int32)
+    table_ref[LIMIT : LIMIT + 1, :] = limit.astype(jnp.int32)
     lane = iota((8, LANES), 1).astype(jnp.bfloat16)
     slot = iota((LANES, LANES), 0).astype(jnp.float32)
     for t in range(tiles):
@@ -70,25 +98,15 @@
         order_ref[t] = dot_t(lane, hit).astype(jnp.int32)
 
 
-def plan(node):
-    tiles = node.shape[0] // LANES
-    return pl.pallas_call(
-        plan_kernel,
-        out_shape=(
-            jax.ShapeDtypeStruct((4 * NODES, LANES), jnp.int32),
-            jax.ShapeDtypeStruct((tiles, 8, LANES), jnp.int32),
-        ),
-        compiler_params=pltpu.CompilerParams(vmem_limit_bytes=16 * 2**20),
-        name="plan",
-    )(node.reshape(tiles, LANES))
-
-
-def place_kernel(table_ref, bins_ref, grads_ref, hess_ref, order_ref, packed_ref, stats_ref):
+def place_kernel(
+    node_ref, bins_ref, grads_ref, hess_ref, packed_ref, stats_ref, plan_ref, order_ref, words_ref, pairs_ref, table_ref, done
+):
     step = pl.program_id(0)
 
     @pl.when(step == 0)
     def _():
-        stats_ref[...] = jnp.zeros_like(stats_ref)
+        plan_ref[...] = jnp.zeros_like(plan_ref)
+        write_plan(node_ref, plan_ref, order_ref)
 
     lane = iota((8, LANES), 1)
     top = iota((8, LANES), 0) == 0
@@ -96,61 +114,87 @@
     for i in range(TILES):
         at = slice(i * LANES, (i + 1) * LANES)
         t = step * TILES + i
-        values = []
+        order = order_ref[t]
         for g in range(groups):
             word = bins_ref[8 * g : 8 * g + 8, at]
             for k in range(1, BYTES):
                 first = 8 * (g + groups * k)
                 word = word | (bins_ref[first : first + 8, at] << (8 * k))
-            values.append(word)
-        grad = jnp.broadcast_to(grads_ref[:, at].astype(jnp.float32), (8, LANES))
-        hess = jnp.broadcast_to(hess_ref[:, at].astype(jnp.float32), (8, LANES))
-        values.append(jnp.where(top, grad, hess))
-        order = order_ref[i]
-        values = [jnp.take_along_axis(v, order, axis=1) for v in values]
+            words_ref[t, 8 * g : 8 * g + 8] = jnp.take_along_axis(word, order, axis=1)
+        grad = jnp.broadcast_to(grads_ref[i : i + 1].astype(jnp.float32), (8, LANES))
+        hess = jnp.broadcast_to(hess_ref[i : i + 1].astype(jnp.float32), (8, LANES))
+        pairs_ref[t] = jnp.take_along_axis(jnp.where(top, grad, hess), order, axis=1)
+
+    @pl.when(step == pl.num_programs(0) - 1)
+    def _():
+        copy = pltpu.make_async_copy(plan_ref, table_ref, done)
+        copy.start()
+        copy.wait()
+
+        def store(tile, values):
+            for g in range(groups):
+                packed_ref[tile, 8 * g : 8 * g + 8] = values[g]
+            stats_ref[tile] = values[groups]
+
+        tiles = words_ref.shape[0]
         for n in range(NODES):
-            dest = table_ref[n, t]
-            count = table_ref[NODES + n, t]
-            start = table_ref[2 * NODES + n, t]
-            tile = dest >> 7
-            off = dest & (LANES - 1)
-            inside = ((lane - off) & (LANES - 1)) < count
-            here = inside & (lane >= off)
-            beyond = inside & (lane < off)
-            for g, value in enumerate(values):
-                moved = pltpu.roll(value, (off - start) & (LANES - 1), axis=1)
-                ref, rows = (packed_ref, slice(8 * g, 8 * g + 8)) if g < groups else (stats_ref, slice(0, 8))
-                pltpu.store(ref.at[tile, rows], moved, mask=here)
-                pltpu.store(ref.at[tile + 1, rows], moved, mask=beyond)
-
-
-def place(table, order, bins, grads, hess):
+
+            def append(t, state):
+                _, held = state
+                dest = table_ref[n, t]
+                count = table_ref[NODES + n, t]
+                start = table_ref[2 * NODES + n, t]
+                off = dest & (LANES - 1)
+                shift = (off - start) & (LANES - 1)
+                full = jnp.broadcast_to(off + count, (8, LANES)) >= LANES
+                filled = lane < off
+                runs = [words_ref[t, 8 * g : 8 * g + 8] for g in range(groups)] + [pairs_ref[t]]
+                runs = [pltpu.roll(run, shift, axis=1) for run in runs]
+                now = [jnp.where(filled, old, run) for old, run in zip(held, runs)]
+                store(dest >> 7, now)
+                return dest + count, tuple(jnp.where(full, run, new) for run, new in zip(runs, now))
+
+            empty = tuple(jnp.zeros((8, LANES), jnp.int32) for _ in range(groups)) + (jnp.zeros((8, LANES), jnp.float32),)
+            last, held = lax.fori_loop(0, tiles, append, (jnp.int32(0), empty), unroll=64)
+            store(last >> 7, held)
+
+
+def place(bins, grads, hess, node):
     features, rows = bins.shape
     tiles = rows // LANES
     room = tiles + 2 * NODES
     words = features // BYTES
-    width = TILES * LANES
-    return pl.pallas_call(
+    table = (4 * NODES, LANES)
+    packed, stats, plan = pl.pallas_call(
         place_kernel,
         grid=(tiles // TILES,),
         in_specs=[
-            pl.BlockSpec(memory_space=pltpu.SMEM),
-            pl.BlockSpec((features, width), lambda i: (0, i)),
-            pl.BlockSpec((1, width), lambda i: (0, i)),
-            pl.BlockSpec((1, width), lambda i: (0, i)),
-            pl.BlockSpec((TILES, 8, LANES), lambda i: (i, 0, 0)),
+            pl.BlockSpec((tiles, LANES), lambda i: (0, 0)),
+            pl.BlockSpec((features, TILES * LANES), lambda i: (0, i)),
+            pl.BlockSpec((TILES, LANES), lambda i: (i, 0)),
+            pl.BlockSpec((TILES, LANES), lambda i: (i, 0)),
         ],
         out_specs=[
             pl.BlockSpec((room, words, LANES), lambda i: (0, 0, 0)),
             pl.BlockSpec((room, 8, LANES), lambda i: (0, 0, 0)),
+            pl.BlockSpec(table, lambda i: (0, 0)),
         ],
         out_shape=[
             jax.ShapeDtypeStruct((room, words, LANES), jnp.int32),
             jax.ShapeDtypeStruct((room, 8, LANES), jnp.float32),
+            jax.ShapeDtypeStruct(table, jnp.int32),
+        ],
+        scratch_shapes=[
+            pltpu.VMEM((tiles, 8, LANES), jnp.int32),
+            pltpu.VMEM((tiles, words, LANES), jnp.int32),
+            pltpu.VMEM((tiles, 8, LANES), jnp.float32),
+            pltpu.SMEM(table, jnp.int32),
+            pltpu.SemaphoreType.DMA(()),
         ],
         compiler_params=pltpu.CompilerParams(vmem_limit_bytes=50 * 2**20),
         name="place",
-    )(table, bins, grads[None], hess[None], order)
+    )(tiled(node), bins, tiled(grads), tiled(hess))
+    return plan, packed, stats
 
 
 def hist_kernel(chunks, per_step, core_ref, table_ref, packed_ref, stats_ref, keep_ref, send_ref, spread_ref, sums_ref):
@@ -162,10 +206,12 @@
 
     @pl.when((pl.program_id(0) == 0) & (pl.program_id(1) == 0))
     def _():
+        lane = iota((1, LANES), 1)
         for c in range(chunks):
             for half in range(CHUNK // LANES):
+                valid = lane + (c * CHUNK + half * LANES) < table_ref[LIMIT, c]
                 for s in range(2):
-                    row = stats_ref[2 * c + half, s : s + 1, :].astype(jnp.bfloat16)
+                    row = jnp.where(valid, stats_ref[2 * c + half, s : s + 1, :], 0.0).astype(jnp.bfloat16)
                     spread_ref[c, HIGH * s : HIGH * (s + 1), half * LANES : (half + 1) * LANES] = jnp.broadcast_to(
                         row, (HIGH, LANES)
                     )
@@ -175,7 +221,7 @@
         raw = jnp.concatenate([packed_ref[2 * c], packed_ref[2 * c + 1]], axis=1)
         grad = spread_ref[c, 0:HIGH]
         hess = spread_ref[c, HIGH:BOTH]
-        n = table_ref[3 * NODES, c]
+        n = table_ref[OWNER, c]
         for q in range(per_step):
             words = raw >> ((pl.program_id(1) * per_step + q) * 8)
             low = (words & (LOW - 1)).astype(jnp.bfloat16)
@@ -238,10 +284,14 @@
     lane_a, lane_b = iota((LANES, LANES), 0), iota((LANES, LANES), 1)
     same_lows = lane_a // LOW == lane_b // LOW
     same_highs = row_a // HIGH == row_b // HIGH
-    within = exact_dot(hist, ones_where(same_lows & (lane_a <= lane_b)))
-    summed = exact_dot(hist, ones_where(same_lows))
-    left = within + exact_dot(ones_where(same_highs & (row_a > row_b)), summed)
-    total = exact_dot(ones_where(same_highs), summed)
+    bf16 = jnp.bfloat16
+    both = jnp.concatenate([ones_where(same_lows & (lane_a <= lane_b), bf16), ones_where(same_lows, bf16)], 1)
+    within = times_ones(hist, both)
+    within, summed = within[:, :LANES], within[:, LANES:]
+    both = jnp.concatenate([ones_where(same_highs & (row_a > row_b), bf16), ones_where(same_highs, bf16)], 0)
+    above = ones_times(both, summed)
+    left = within + above[:rows]
+    total = above[rows:]
     left = left.reshape(NODES // 2, 2, HIGH, LANES)
     total = total.reshape(NODES // 2, 2, HIGH, LANES)
     grad_left, hess_left = left[:, 0], left[:, 1]
@@ -260,8 +310,8 @@
     own_high = iota((NODES // 2 * HIGH, BINS), 0) % HIGH == iota((NODES // 2 * HIGH, BINS), 1) // LOW
     for odd in range(2):
         for slot in range(SHARE):
-            take = ones_where(from_lane == (odd * SHARE + slot) * LOW + to_bin % LOW)
-            spread = jnp.where(own_high, exact_dot(gain, take), 0.0)
+            take = ones_where(from_lane == (odd * SHARE + slot) * LOW + to_bin % LOW, bf16)
+            spread = jnp.where(own_high, times_ones(gain, take), 0.0)
             rows_out = jnp.sum(spread.reshape(NODES // 2, HIGH, BINS), axis=1)
             for pair in range(NODES // 2):
                 gain_ref[slot, 2 * pair + odd] = rows_out[pair]
@@ -286,8 +336,7 @@
     swap = [(i, i ^ 1) for i in range(row_size)]
     same_core = [[chip * CORES + c for chip in range(row_size // CORES)] for c in range(CORES)]
     core = (lax.axis_index("row") % CORES)[None]
-    table, order = plan(node)
-    packed, stats = place(table, order, bins, grads, hess)
+    table, packed, stats = place(bins, grads, hess, node)
     keep, send = histogram(core, table, packed, stats, bins.shape[1])
     pair = keep + lax.ppermute(send, "row", swap)
     gain, own_best = gains(lax.all_to_all(pair, "row", 0, 0, axis_index_groups=same_core, tiled=True))

time: 91.8 us -> 87.7 us (0.955)
  local copies, waits for them, and re-layouts: 2.42 us -> 0.19 us
  Pallas kernels: 35.2 us -> 33.5 us
    pallas_call x1 -> x0, Pallas kernels: 1.54 us -> none  [plan(): pl.pallas_call(plan_kernel, out_shape=(jax.ShapeDtypeStruct((4 * NODES, L...]
    broadcast_in_dim x2 -> x0, local copies, waits for them, and re-layouts: 1.48 us -> none  [the longest x1 0.74 us: place(): hess[None]]
where the time goes in v5:
time: 87.7 us; the launch traced here: 87.5 us
  blocking collectives  46.3 us (53%)
  Pallas kernels  33.5 us (38%)
  starting transfers between devices  3.35 us (4%)
  waiting for transfers between devices  2.29 us (3%)
  other arithmetic  1.2 us (1%)
    all_to_all x1, blocking collectives, per_device(): lax.all_to_all(copies, ('row', 'feat'), 0, 0, tiled=True)  25.5 us
    pallas_call x1, Pallas kernels, histogram(): pl.pallas_call(functools.partial(hist_kernel, chunks, per_step), grid=(bl...  24.1 us
    all_to_all x1, blocking collectives, per_device(): lax.all_to_all(pair, 'row', 0, 0, axis_index_groups=same_core, tiled=True)  20.8 us
    pallas_call x1, Pallas kernels, place(): pl.pallas_call(place_kernel, grid=(tiles // TILES,), in_specs=[pl.BlockSp...  8.5 us
    ppermute x1, starting transfers between devices, per_device(): pair = keep + lax.ppermute(send, 'row', swap)  3.35 us
    ppermute x1, waiting for transfers between devices, per_device(): pair = keep + lax.ppermute(send, 'row', swap)  2.29 us
  transfers between devices with their start and end apart: 1, of which 1 were waited for; matrix products, arithmetic and copies ran while one was open for 0% of the time, Pallas kernels for 0%

profile of v5, /device:TPU:1, one launch (start us, length us, event | category | flops | bytes accessed | tf_op | source)
XLA Modules:
  0.0 87.5 jit_solution(17889047487380643850)
XLA Ops:
  0.6 8.5 %place.1 = (s32[80,32,128]{2,1,0:T(8,128)S(1)}, f32[80,8,128]{2,1,0:T(8,128)S(1)}, s32[32,128]{1,0:T(8,128)S(1)}) custom-call(s32[64,128]{1,0:T(8,128)} %bitcast.10, s32[128,8192]{1,0:T(8,128)} %bins_ref.1, bf16[64,128]{1,0:T(8,128)(2,1)} %bitcast.11, bf16[64,128]{1,0:T(8,128)(2,1)} %bitcast.12), custom_call_target="tpu_custom_call" | custom-call | tf_op jit(solution)/shard_map/place/pallas_call | solution.py:168
  9.2 24.1 %histogram.1 = (f32[4,4,4,32,128]{4,3,2,1,0:T(8,128)S(1)}, f32[4,4,4,32,128]{4,3,2,1,0:T(8,128)S(1)}) custom-call(s32[1]{0:T(128)} %bitcast.core_ref, s32[32,128]{1,0:T(8,128)S(1)} %get-tuple-element.9.table_ref, s32[80,32,128]{2,1,0:T(8,128)S(1)} %get-tuple-element.10.packed_ref, f32[80,8,128]{2,1,0:T(8,128)S(1)} %get-tuple-element.11.stats_ref), custom_call_target="tpu_custom_call" | custom-call | tf_op jit(solution)/shard_map/histogram/pallas_call | solution.py:257
  33.3 3.3 %collective-permute-start = (f32[16,4,32,128]{3,2,1,0:T(8,128)S(1)}, f32[16,4,32,128]{3,2,1,0:T(8,128)S(1)}, u32[]{:S(2)}, u32[]{:S(2)}) collective-permute-start(f32[16,4,32,128]{3,2,1,0:T(8,128)S(1)} %bitcast.9), channel_id=1, source_target_pairs={{0,8},{8,0},{16,24},{24,16},{32,40},{40,32},{48,56},{56,48},{64,72... | collective-permute-start | bytes 3145736 | tf_op jit(solution)/shard_map/ppermute | solution.py:341
  36.7 2.3 %collective-permute-done = f32[16,4,32,128]{3,2,1,0:T(8,128)S(1)} collective-permute-done((f32[16,4,32,128]{3,2,1,0:T(8,128)S(1)}, f32[16,4,32,128]{3,2,1,0:T(8,128)S(1)}, u32[]{:S(2)}, u32[]{:S(2)}) %collective-permute-start) | collective-permute-done | bytes 1048608 | tf_op jit(solution)/shard_map/ppermute | solution.py:341
  38.9 0.2 bitcast_add_fusion
  39.2 20.8 %all_to_all.11 = f32[16,4,32,128]{3,2,1,0:T(8,128)S(1)} all-to-all(f32[16,4,32,128]{3,2,1,0:T(8,128)S(1)} %bitcast_add_fusion), channel_id=1, replica_groups={{0,16,32,48,64,80,96,112,128,144,160,176,192,208,224,240},{8,24,40,56,7..., dimensions={0} | all-to-all | bytes 2097152 | tf_op jit(solution)/shard_map/all_to_all | solution.py:342
  59.9 0.8 gains.1
  60.8 0.1 slice_reduce_fusion
  60.9 0.1 broadcast_in_dim.11
  61.0 25.5 %all_to_all.12 = f32[256,1,8]{2,1,0:T(1,128)S(1)} all-to-all(f32[256,1,8]{2,1,0:T(1,128)S(1)} %broadcast_in_dim.11), channel_id=1, replica_groups=mesh['row'=32,'feat'=8] {'row','feat'}, dimensions={0} | all-to-all | bytes 16384 | tf_op jit(solution)/shard_map/all_to_all | solution.py:344
  86.5 0.3 reduce_max.9
  86.8 0.0 copy-start
  86.8 0.7 broadcast_subtract_fusion
  87.5 0.0 copy-done
Async XLA Ops:
  33.3 5.6 %collective-permute-start = (f32[16,4,32,128]{3,2,1,0:T(8,128)S(1)}, f32[16,4,32,128]{3,2,1,0:T(8,128)S(1)}, u32[]{:S(2)}, u32[]{:S(2)}) collective-permute-start(f32[16,4,32,128]{3,2,1,0:T(8,128)S(1)} %bitcast.9), channel_id=1, source_target_pairs={{0,8},{8,0},{16,24},{24,16},{32,40},{40,32},{48,56},{56,48},{64,72... | collective-permute-start | bytes 3145736 | tf_op jit(solution)/shard_map/ppermute | solution.py:341
  86.8 0.7 copy-start

commit v6 on v5

--- a/solution.py
+++ b/solution.py
@@ -16,7 +16,7 @@
 CORES = 2
 SHARE = 4
 BYTES = 4
-TILES = 16
+TILES = 64
 OWNER = 3 * NODES
 LIMIT = OWNER + 1
 BOTH = 2 * HIGH

time: 87.7 us -> 85.7 us (0.977)
  Pallas kernels: 33.5 us -> 31.6 us
    pallas_call x1, Pallas kernels: 8.5 us -> 6.62 us  [place(): pl.pallas_call(place_kernel, grid=(tiles // TILES,), in_specs=[pl.BlockSp...]
where the time goes in v6:
time: 85.7 us; the launch traced here: 85.6 us
  blocking collectives  46.3 us (54%)
  Pallas kernels  31.6 us (37%)
  starting transfers between devices  3.3 us (4%)
  waiting for transfers between devices  2.29 us (3%)
  other arithmetic  1.2 us (1%)
    all_to_all x1, blocking collectives, per_device(): lax.all_to_all(copies, ('row', 'feat'), 0, 0, tiled=True)  25.5 us
    pallas_call x1, Pallas kernels, histogram(): pl.pallas_call(functools.partial(hist_kernel, chunks, per_step), grid=(bl...  24.2 us
    all_to_all x1, blocking collectives, per_device(): lax.all_to_all(pair, 'row', 0, 0, axis_index_groups=same_core, tiled=True)  20.8 us
    pallas_call x1, Pallas kernels, place(): pl.pallas_call(place_kernel, grid=(tiles // TILES,), in_specs=[pl.BlockSp...  6.62 us
    ppermute x1, starting transfers between devices, per_device(): pair = keep + lax.ppermute(send, 'row', swap)  3.3 us
    ppermute x1, waiting for transfers between devices, per_device(): pair = keep + lax.ppermute(send, 'row', swap)  2.29 us
  transfers between devices with their start and end apart: 1, of which 1 were waited for; matrix products, arithmetic and copies ran while one was open for 0% of the time, Pallas kernels for 0%

profile of v6, /device:TPU:1, one launch (start us, length us, event | category | flops | bytes accessed | tf_op | source)
XLA Modules:
  0.0 85.6 jit_solution(13664905058061212690)
XLA Ops:
  0.6 6.6 %place.1 = (s32[80,32,128]{2,1,0:T(8,128)S(1)}, f32[80,8,128]{2,1,0:T(8,128)S(1)}, s32[32,128]{1,0:T(8,128)S(1)}) custom-call(s32[64,128]{1,0:T(8,128)} %bitcast.10, s32[128,8192]{1,0:T(8,128)} %bins_ref.1, bf16[64,128]{1,0:T(8,128)(2,1)} %bitcast.11, bf16[64,128]{1,0:T(8,128)(2,1)} %bitcast.12), custom_call_target="tpu_custom_call" | custom-call | tf_op jit(solution)/shard_map/place/pallas_call | solution.py:168
  7.3 24.2 %histogram.1 = (f32[4,4,4,32,128]{4,3,2,1,0:T(8,128)S(1)}, f32[4,4,4,32,128]{4,3,2,1,0:T(8,128)S(1)}) custom-call(s32[1]{0:T(128)} %bitcast.core_ref, s32[32,128]{1,0:T(8,128)S(1)} %get-tuple-element.9.table_ref, s32[80,32,128]{2,1,0:T(8,128)S(1)} %get-tuple-element.10.packed_ref, f32[80,8,128]{2,1,0:T(8,128)S(1)} %get-tuple-element.11.stats_ref), custom_call_target="tpu_custom_call" | custom-call | tf_op jit(solution)/shard_map/histogram/pallas_call | solution.py:257
  31.4 3.3 %collective-permute-start = (f32[16,4,32,128]{3,2,1,0:T(8,128)S(1)}, f32[16,4,32,128]{3,2,1,0:T(8,128)S(1)}, u32[]{:S(2)}, u32[]{:S(2)}) collective-permute-start(f32[16,4,32,128]{3,2,1,0:T(8,128)S(1)} %bitcast.9), channel_id=1, source_target_pairs={{0,8},{8,0},{16,24},{24,16},{32,40},{40,32},{48,56},{56,48},{64,72... | collective-permute-start | bytes 3145736 | tf_op jit(solution)/shard_map/ppermute | solution.py:341
  34.7 2.3 %collective-permute-done = f32[16,4,32,128]{3,2,1,0:T(8,128)S(1)} collective-permute-done((f32[16,4,32,128]{3,2,1,0:T(8,128)S(1)}, f32[16,4,32,128]{3,2,1,0:T(8,128)S(1)}, u32[]{:S(2)}, u32[]{:S(2)}) %collective-permute-start) | collective-permute-done | bytes 1048608 | tf_op jit(solution)/shard_map/ppermute | solution.py:341
  37.0 0.2 bitcast_add_fusion
  37.3 20.8 %all_to_all.11 = f32[16,4,32,128]{3,2,1,0:T(8,128)S(1)} all-to-all(f32[16,4,32,128]{3,2,1,0:T(8,128)S(1)} %bitcast_add_fusion), channel_id=1, replica_groups={{0,16,32,48,64,80,96,112,128,144,160,176,192,208,224,240},{8,24,40,56,7..., dimensions={0} | all-to-all | bytes 2097152 | tf_op jit(solution)/shard_map/all_to_all | solution.py:342
  58.1 0.8 gains.1
  58.9 0.1 slice_reduce_fusion
  59.0 0.1 broadcast_in_dim.11
  59.1 25.5 %all_to_all.12 = f32[256,1,8]{2,1,0:T(1,128)S(1)} all-to-all(f32[256,1,8]{2,1,0:T(1,128)S(1)} %broadcast_in_dim.11), channel_id=1, replica_groups=mesh['row'=32,'feat'=8] {'row','feat'}, dimensions={0} | all-to-all | bytes 16384 | tf_op jit(solution)/shard_map/all_to_all | solution.py:344
  84.6 0.3 reduce_max.9
  84.9 0.0 copy-start
  84.9 0.7 broadcast_subtract_fusion
  85.6 0.0 copy-done
Async XLA Ops:
  31.4 5.6 %collective-permute-start = (f32[16,4,32,128]{3,2,1,0:T(8,128)S(1)}, f32[16,4,32,128]{3,2,1,0:T(8,128)S(1)}, u32[]{:S(2)}, u32[]{:S(2)}) collective-permute-start(f32[16,4,32,128]{3,2,1,0:T(8,128)S(1)} %bitcast.9), channel_id=1, source_target_pairs={{0,8},{8,0},{16,24},{24,16},{32,40},{40,32},{48,56},{56,48},{64,72... | collective-permute-start | bytes 3145736 | tf_op jit(solution)/shard_map/ppermute | solution.py:341
  84.9 0.7 copy-start
